TPU v7x, 256 devices: a whole 4x4x8 slice. The times are simulated.
256 devices in a mesh: grp: 4 (over z_lo, core), fsdp: 64 (over z_hi, x, y).
Axes of the slice: x: 4, y: 4, z: 8 (z_hi: 4, z_lo: 2; z = z_hi * 2 + z_lo), core: 2. Of those that a mesh axis runs over, the one named last changes fastest.
Arguments:
- layer_input_rows: bfloat16 [131072, 8192], P(('grp', 'fsdp')), may hold values from -400 to 400, as said below
- input_norm_gain: bfloat16 [8192], replicated, may hold values from 0.5 to 1.5
- key_value_codes: int32 [8192, 256], P('fsdp'), may hold values from 0 to 65535
- block_scale_codes: int32 [256, 128], P('fsdp'), may hold values from -2147483648 to 2147483646
- outer_scale_codes: int32 [512], P('fsdp'), may hold values from 0 to 255
- adapter_down_factor: bfloat16 [8192, 64], replicated, may hold values from -0.0625 to 0.0625
- adapter_up_factor: bfloat16 [64, 1024], replicated, may hold values from -0.75 to 0.75
- target: bfloat16 [131072, 1024], P(('grp', 'fsdp')), may hold values from -18 to 18
Outputs:
- kv: bfloat16 [131072, 1024], P(('grp', 'fsdp'))
- loss: float32 [], replicated
Inputs may be any that keep to these rules, and one draw needn't show every extreme that they name: layer_input_rows rows and features carry varied scales.
All inputs are finite; a program needn't handle non-finite values.
Results may differ from a plain program's by a relative error of at most 0.0057.
Values may be sent and summed in bfloat16 or wider, within the bound.
No kernel may reach another device: no remote copies, remote signals or barrier semaphores. Data moves between devices by JAX's collectives and lax.ppermute only.
A program may use at most 128 MiB of HBM per device.

v0:
```python
import jax
import jax.numpy as jnp
from jax import lax
from jax.sharding import PartitionSpec as P

adapter_scale = 0.25
epsilon = 1e-06
nf4_levels = (
    -1.0,
    -0.6961928009986877,
    -0.5250730514526367,
    -0.39491748809814453,
    -0.28444138169288635,
    -0.18477343022823334,
    -0.09105003625154495,
    0.0,
    0.07958029955625534,
    0.16093020141124725,
    0.24611230194568634,
    0.33791524171066284,
    0.44070982933044434,
    0.5626170039176941,
    0.7229568362236023,
    1.0,
)


def copy_for_each(value, axis):
    length = lax.axis_size(axis)
    return lax.all_to_all(
        jnp.broadcast_to(value[None], (length, *value.shape)), axis, 0, 0, tiled=True
    )


def taken_together(value, axis):
    everything = copy_for_each(value, axis)
    return jnp.sum(everything, axis=0)


def unpack_scales(code_words, outer_scale_codes, all_rows):
    per_row = code_words.size // all_rows
    flat = code_words.reshape(all_rows, per_row)
    shifts = jnp.arange(4, dtype=jnp.int32) * 8
    code_bytes = jnp.bitwise_and(jnp.right_shift(flat[:, :, None], shifts[None, None, :]), 255)
    code_bytes = code_bytes.reshape(all_rows, per_row * 4).astype(jnp.float32)
    group_rows = all_rows // outer_scale_codes.shape[0]
    second = jnp.exp2(outer_scale_codes.astype(jnp.float32) / 128.0 - 6.0)
    second = jnp.repeat(second, group_rows)
    return (code_bytes + 0.5) / 256.0 * second[:, None]


def decode_codes(words, absmax):
    height = words.shape[0]
    shifts = jnp.arange(4, dtype=jnp.int32) * 4
    nibbles = jnp.bitwise_and(jnp.right_shift(words[:, :, None], shifts[None, None, :]), 15)
    nibbles = nibbles.reshape(height, words.shape[1] * 4)
    values = jnp.zeros(nibbles.shape, jnp.float32)
    for number, level in enumerate(nf4_levels):
        values = jnp.where(nibbles == number, jnp.float32(level), values)
    width = values.shape[1]
    count = absmax.shape[1]
    scaled = values.reshape(height, count, width // count) * absmax[:, :, None]
    return scaled.reshape(height, width).astype(jnp.bfloat16)


def apply_input_norm(input_states, input_norm_gain):
    values = input_states.astype(jnp.float32)
    inverse = lax.rsqrt(jnp.mean(values * values, axis=1, keepdims=True) + epsilon)
    return (values * inverse * input_norm_gain.astype(jnp.float32)[None, :]).astype(jnp.bfloat16)


def per_device(
    layer_input_rows,
    input_norm_gain,
    key_value_codes,
    block_scale_codes,
    outer_scale_codes,
    adapter_down_factor,
    adapter_up_factor,
    target,
):
    normed_input = apply_input_norm(layer_input_rows, input_norm_gain)
    rows_dev = key_value_codes.shape[0]
    columns = key_value_codes.shape[1] * 4
    owned = decode_codes(
        key_value_codes, unpack_scales(block_scale_codes, outer_scale_codes, rows_dev)
    )
    frozen_output = jnp.dot(
        normed_input,
        lax.all_gather(owned, "fsdp", axis=0, tiled=True),
        preferred_element_type=jnp.float32,
    )
    adapter_output = jnp.dot(
        normed_input, adapter_down_factor, preferred_element_type=jnp.float32
    ).astype(jnp.bfloat16)
    precise_output = frozen_output + adapter_scale * jnp.dot(
        adapter_output, adapter_up_factor, preferred_element_type=jnp.float32
    )
    error_terms = precise_output - target.astype(jnp.float32)
    partial_value = jnp.sum(error_terms * error_terms) / (
        normed_input.shape[0] * lax.axis_size("fsdp") * columns
    )
    group_total = taken_together(partial_value, "fsdp")
    loss = taken_together(group_total, "grp")
    return (precise_output.astype(jnp.bfloat16), loss)


def solution(mesh):
    placed = (
        P(("grp", "fsdp"), None),
        P(),
        P("fsdp", None),
        P("fsdp", None),
        P("fsdp"),
        P(),
        P(),
        P(("grp", "fsdp"), None),
    )
    return jax.shard_map(
        per_device,
        mesh=mesh,
        in_specs=placed,
        out_specs=(P(("grp", "fsdp"), None), P()),
        check_vma=False,
    )
```

profile of v0, /device:TPU:1, one launch (start us, length us, event | category | flops | bytes accessed | tf_op | source)
XLA Modules:
  0.0 304.2 jit_solution(3043209159881507789)
XLA Ops:
  7.2 0.0 copy-start
  7.2 0.0 copy-start.2
  7.2 0.0 all-gather.2.cloned.1.call-start
  7.3 0.7 exponential_multiply_fusion
  8.0 0.1 shift_right_arithmetic.58
  8.1 0.1 broadcast_in_dim.87
  8.2 0.1 mul.80
  8.2 0.8 shift_right_arithmetic.54
  9.0 0.1 copy.15
  9.1 0.1 shift_right_arithmetic.51
  9.3 1.0 copy.14
  10.3 0.1 add_multiply_fusion
  10.3 0.1 shift_right_arithmetic.48
  10.4 1.4 fusion.15
  11.8 0.0 all-gather.2.cloned.1.call-update
  11.9 0.7 convert_element_type.32
  12.6 5.1 %fusion = f32[512]{0:T(512)S(1)} fusion(bf16[512,8192]{1,0:T(8,128)(2,1)} %param.8), kind=kLoop, calls=%fused_computation.2 | loop fusion | flops 12582400 | bytes 8390656 | tf_op jit(solution)/shard_map/reduce_sum | solution.py:68
  17.7 0.0 copy-start.1
  17.7 0.0 copy-done
  17.7 0.0 copy-done.2
  17.7 7.9 %fusion.13 = f32[512,1024]{1,0:T(8,128)} fusion(bf16[64,1024]{1,0:T(8,128)(2,1)S(1)} %copy-done.2, bf16[8192,64]{0,1:T(8,128)(2,1)S(1)} %copy-done, bf16[512,8192]{1,0:T(8,128)(2,1)} %param.8, f32[8192]{0:T(1024)S(1)} %convert_element_type.32, f32[512]{0:T(512)S(1)} %add_rsqrt_fusion), kind=kOutput, calls=%fused_computation.10 | convolution fusion | flops 620789760 | bytes 11700224 | tf_op jit(solution)/shard_map/dot_general | solution.py:96
  25.6 223.1 %all-gather.2.cloned.1.call-done = bf16[8192,1024]{0,1:T(8,128)(2,1)} async-done(((bf16[128,1024]{0,1:T(8,128)(2,1)}), bf16[8192,1024]{0,1:T(8,128)(2,1)}) %all-gather.2.cloned.1.call-update) | async-done | bytes 16777232 | tf_op jit(solution)/shard_map/all_gather | solution.py:90
  248.7 0.0 copy-done.1
  248.7 16.8 %multiply_reduce_fusion = (f32[]{:T(128)}, bf16[512,1024]{1,0:T(8,128)(2,1)}) fusion(bf16[512,1024]{1,0:T(8,128)(2,1)S(1)} %copy-done.1, f32[512,1024]{1,0:T(8,128)} %fusion.13, bf16[8192,1024]{0,1:T(8,128)(2,1)} %all-gather.2.cloned.1.call-done, bf16[512,8192]{1,0:T(8,128)(2,1)} %param.8, f32[8192]{0:T(1024)S(1)} %convert_element_type.32, ...), kind=kOutput, calls=%fused_computation.7 | convolution fusion | flops 8610381824 | bytes 29394948 | tf_op jit(solution)/shard_map/dot_general | solution.py:88
  266.2 19.4 %all_to_all.12 = f32[64,1,1]{2,1,0:T(1,128)S(1)} all-to-all(f32[64,1,1]{2,1,0:T(1,128)S(1)} %broadcast_in_dim.88), channel_id=1, replica_groups=mesh['grp'=4,'fsdp'=64] {'fsdp'}, dimensions={0} | all-to-all | bytes 512 | tf_op jit(solution)/shard_map/all_to_all | solution.py:30
  285.5 0.7 reduce_sum.38
  286.2 0.6 broadcast_in_dim.89
  286.9 9.9 %all_to_all.13 = f32[4,1,1]{2,1,0:T(1,128)S(1)} all-to-all(f32[4,1,1]{2,1,0:T(1,128)S(1)} %broadcast_in_dim.89), channel_id=1, replica_groups=mesh['grp'=4,'fsdp'=64] {'grp'}, dimensions={0} | all-to-all | bytes 32 | tf_op jit(solution)/shard_map/all_to_all | solution.py:30
  296.7 0.6 reduce_sum.39
  (7 shorter events, 0.1 us)
Async XLA Ops:
  7.2 10.6 %copy-start = (bf16[8192,64]{0,1:T(8,128)(2,1)S(1)}, bf16[8192,64]{0,1:T(8,128)(2,1)}, u32[]{:S(2)}) copy-start(bf16[8192,64]{0,1:T(8,128)(2,1)} %param.13) | copy-start | bytes 3145732
  7.2 10.6 %copy-start.2 = (bf16[64,1024]{1,0:T(8,128)(2,1)S(1)}, bf16[64,1024]{1,0:T(8,128)(2,1)}, u32[]{:S(2)}) copy-start(bf16[64,1024]{1,0:T(8,128)(2,1)} %param.14) | copy-start | bytes 393220
  7.2 241.5 %all-gather.2.cloned.1.call-start = ((), (), s32[]{:S(2)}) async-start(), calls=%async_computation.2 | async-start | bytes 17039360 | tf_op jit(solution)/shard_map/all_gather | solution.py:90
  17.7 231.0 %copy-start.1 = (bf16[512,1024]{1,0:T(8,128)(2,1)S(1)}, bf16[512,1024]{1,0:T(8,128)(2,1)}, u32[]{:S(2)}) copy-start(bf16[512,1024]{1,0:T(8,128)(2,1)} %param.15) | copy-start | bytes 3145732
Sparse Core Ops, SparseCore 0:
  12.0 236.6 all-gather.1
where the time goes:
time: 304 us
  waiting for transfers between devices  223 us (73%)
  blocking collectives  29.2 us (10%)
  matrix products  24.7 us (8%)
  between operations  14.8 us (5%)
  other arithmetic  9.34 us (3%)
    all_gather x1, waiting for transfers between devices, per_device(): lax.all_gather(owned, 'fsdp', axis=0, tiled=True)  223 us
    all_to_all x2, blocking collectives, copy_for_each(): lax.all_to_all(jnp.broadcast_to(value[None], (length, *value.shape)), axi...  29.2 us
    dot_general x1, matrix products, per_device(): jnp.dot(normed_input, lax.all_gather(owned, 'fsdp', axis=0, tiled=True),...  16.8 us
    dot_general x1, matrix products, per_device(): jnp.dot(adapter_output, adapter_up_factor, preferred_element_type=jnp.flo...  7.88 us
  transfers between devices with their start and end apart: 1, of which 1 were waited for; matrix products, arithmetic and copies ran while one was open for 5% of the time, Pallas kernels for 0%

commit v1 on v0

v1 whole, which is shorter than its diff:
```python
import functools

import numpy as np

import jax
import jax.numpy as jnp
from jax import lax
from jax.experimental import pallas as pl
from jax.experimental.pallas import tpu as pltpu
from jax.sharding import PartitionSpec as P

adapter_scale = 0.25
epsilon = 1e-06
nf4_levels = (
    -1.0,
    -0.6961928009986877,
    -0.5250730514526367,
    -0.39491748809814453,
    -0.28444138169288635,
    -0.18477343022823334,
    -0.09105003625154495,
    0.0,
    0.07958029955625534,
    0.16093020141124725,
    0.24611230194568634,
    0.33791524171066284,
    0.44070982933044434,
    0.5626170039176941,
    0.7229568362236023,
    1.0,
)

AXES = ("grp", "fsdp")
LANES = 128
PART = 256
HALF = 2 * PART


def permutation(move):
    sizes = (2, 2, 4, 4, 4)
    pairs = []
    for source in range(int(np.prod(sizes))):
        place = [int(v) for v in np.unravel_index(source, sizes)]
        target = [v % s for v, s in zip(move(*place), sizes)]
        pairs.append((source, int(np.ravel_multi_index(target, sizes))))
    return pairs


def along(axis, step):
    def move(*place):
        place = list(place)
        place[axis] += step if place[1] == 0 else -step
        return place

    return permutation(move)


ZH, X, Y = 2, 3, 4
FORWARD = {axis: along(axis, 1) for axis in (ZH, X, Y)}
BACKWARD = {axis: along(axis, -1) for axis in (ZH, X, Y)}
ORDER = ((Y, X), (X, Y))
OTHER_CORE = permutation(lambda zl, c, zh, x, y: (zl, 1 - c, zh, x, y))


def ring(block, axis):
    behind = lax.ppermute(block, AXES, FORWARD[axis])
    ahead = lax.ppermute(block, AXES, BACKWARD[axis])
    opposite = lax.ppermute(behind, AXES, FORWARD[axis])
    return [block, behind, ahead, opposite]


_DEVICES = np.arange(256).reshape(16, 16)
LOSS_GROUPS = (_DEVICES.tolist(), _DEVICES.T.tolist())


def decode_kernel(place, outer, words, scale_words, gain, down, up, whole, levels):
    core = place[0]
    words_t = jnp.transpose(words[...])
    for j in range(4):
        code = jnp.bitwise_and(jnp.right_shift(words_t, 4 * j), 15)
        value = jnp.full(code.shape, nf4_levels[0], jnp.float32)
        for number in range(1, 16):
            value = jnp.where(code == number, jnp.float32(nf4_levels[number]), value)
        levels[pl.ds(j, LANES, stride=4), :] = value
    row = lax.broadcasted_iota(jnp.int32, (1, LANES), 1)
    second = jnp.zeros((1, LANES), jnp.float32)
    for g in range(8):
        code = outer[g].astype(jnp.float32)
        second = jnp.where(row // 16 == g, code, second)
    second = jnp.exp2(second / 128.0 - 6.0)
    code_bytes = jnp.concatenate(
        [
            jnp.bitwise_and(jnp.right_shift(scale_words[...], 8 * j), 255).astype(jnp.float32)
            for j in range(4)
        ],
        axis=0,
    ).astype(jnp.bfloat16)
    word_at = lax.broadcasted_iota(jnp.int32, (LANES, LANES), 0)
    row_at = lax.broadcasted_iota(jnp.int32, (LANES, LANES), 1)
    which = lax.broadcasted_iota(jnp.int32, (4, LANES), 0)
    own_rows = which == lax.broadcasted_iota(jnp.int32, (4, LANES), 1) // 32
    adapter = lax.dot_general(
        up[...], down[...], (((0,), (0,)), ((), ())), preferred_element_type=jnp.float32
    )
    gain_row = gain[0].astype(jnp.float32)
    pieces = []
    for q in range(2):
        pick = (word_at == 4 * (row_at % 32) + (2 * core + q)).astype(jnp.float32)
        found = jnp.dot(
            code_bytes, pick.astype(jnp.bfloat16), preferred_element_type=jnp.float32
        )
        for j in range(4):
            code = jnp.sum(
                jnp.where(own_rows, found[4 * j : 4 * j + 4], 0.0), axis=0, keepdims=True
            )
            absmax = (code + 0.5) / 256.0 * second
            block = 4 * q + j
            rows = slice(64 * block, 64 * block + 64)
            weight = levels[rows, :] * absmax + adapter_scale * adapter[rows]
            pieces.append((weight * gain_row).astype(jnp.bfloat16))
    whole[...] = jnp.concatenate(pieces, axis=0)


def decode(place, words, scale_words, outer, gain, down, up):
    grid = pltpu.PrefetchScalarGridSpec(
        num_scalar_prefetch=2,
        grid=(1,),
        in_specs=[
            pl.BlockSpec((LANES, LANES), lambda i, p, o: (0, p[0])),
            pl.BlockSpec((4, LANES), lambda i, p, o: (0, 0)),
            pl.BlockSpec((1, 1, LANES), lambda i, p, o: (p[1], 0, 0)),
            pl.BlockSpec((64, LANES), lambda i, p, o: (0, p[1])),
            pl.BlockSpec((64, HALF), lambda i, p, o: (0, p[0])),
        ],
        out_specs=pl.BlockSpec((HALF, LANES), lambda i, p, o: (0, 0)),
        scratch_shapes=[pltpu.VMEM((HALF, LANES), jnp.float32)],
    )
    return pl.pallas_call(
        decode_kernel,
        grid_spec=grid,
        out_shape=jax.ShapeDtypeStruct((HALF, LANES), jnp.bfloat16),
    )(place, outer, words, scale_words, gain.reshape(64, 1, LANES), down.T, up)


def ring_offset(core, j):
    step = 1 - 2 * core
    return jnp.where(j == 0, 0, jnp.where(j == 1, -step, jnp.where(j == 2, step, 2)))


def squares_kernel(x, squares):
    def rows(i, carry):
        at = pl.ds(pl.multiple_of(i * 16, 16), 16)
        sums = jnp.zeros((16, LANES), jnp.float32)
        for k in range(x.shape[1] // LANES):
            v = x[at, k * LANES : (k + 1) * LANES].astype(jnp.float32)
            sums += v * v
        squares[at, :] = sums
        return carry

    lax.fori_loop(0, x.shape[0] // 16, rows, 0)


def sum_squares(x):
    tokens, width = x.shape
    return pl.pallas_call(
        squares_kernel,
        grid=(8,),
        in_specs=[pl.BlockSpec((tokens // 8, width), lambda i: (i, 0))],
        out_specs=pl.BlockSpec((tokens // 8, LANES), lambda i: (i, 0)),
        out_shape=jax.ShapeDtypeStruct((tokens, LANES), jnp.float32),
        cost_estimate=pl.CostEstimate(
            flops=2 * tokens * width, transcendentals=0, bytes_accessed=2 * tokens * width
        ),
    )(x)


class Products:
    def __init__(self, arrivals, x, weights, x_space, w_space, x_sem, w_sem):
        core = lax.axis_index("grp") % 2
        own = lax.axis_index("fsdp")
        position = {ZH: own // 16, X: (own // 4) % 4, Y: own % 4}
        stride = {ZH: 16, X: 4, Y: 1}

        def base(axis, j):
            return (position[axis] + ring_offset(core, j)) % 4 * stride[axis]

        self.x_space, self.w_space, self.x_sem, self.w_sem = x_space, w_space, x_sem, w_sem
        self.weights = weights
        self.chunks = [(j, part) for j in arrivals for part in range(2)]
        tokens = x[0].shape[0]
        for chunk, (j, part) in enumerate(self.chunks):
            self.weight_copy(chunk).start()
            middle, last = ORDER[part]
            width = 4 * LANES if middle == Y else LANES
            for spot in range(0, 16 * LANES, width):
                shard = spot // (4 * LANES) * 16 + spot // LANES % 4 * stride[middle]
                source = pl.multiple_of((shard + base(last, j)) * LANES, LANES)
                for half in range(2):
                    pltpu.make_async_copy(
                        x[half].at[:, pl.ds(source, width)],
                        x_space.at[chunk, pl.ds(half * tokens, tokens), pl.ds(spot, width)],
                        x_sem.at[chunk],
                    ).start()

        def slot(axis, place):
            ahead = (place - position[axis]) % 4
            step = (1 - 2 * core) % 4
            return jnp.where(
                ahead == 0, 0, jnp.where(ahead == 2, 3, jnp.where(ahead == step, 2, 1))
            )

        self.slots = [
            [slot(middle, m) * 4 + slot(ZH, zh) for zh in range(4) for m in range(4)]
            for middle, _ in ORDER
        ]

    def weight_copy(self, chunk):
        return pltpu.make_async_copy(
            self.weights[chunk], self.w_space.at[chunk], self.w_sem.at[chunk]
        )

    def wait(self, chunk):
        space = self.x_space.at[chunk]
        pltpu.make_async_copy(space, space, self.x_sem.at[chunk]).wait()
        self.weight_copy(chunk).wait()

    def product(self, chunk, rows):
        slots = self.slots[self.chunks[chunk][1]]
        right = jnp.concatenate([self.w_space[chunk, slot] for slot in slots], axis=1)
        return lax.dot_general(
            self.x_space[chunk, rows, :],
            right,
            (((1,), (1,)), ((), ())),
            preferred_element_type=jnp.float32,
        )


ROWS = 256


def add_kernel(arrivals, *refs):
    first = 0 in arrivals
    count = 2 * len(arrivals)
    x, refs = refs[:2], refs[2:]
    weights, refs = refs[:count], refs[count:]
    if not first:
        before, refs = refs[0], refs[1:]
    out, x_space, w_space, total, x_sem, w_sem, sem = refs
    if not first:
        bring = pltpu.make_async_copy(before, total, sem)
        bring.start()
    products = Products(arrivals, x, weights, x_space, w_space, x_sem, w_sem)
    if not first:
        bring.wait()
    for chunk, (j, part) in enumerate(products.chunks):
        products.wait(chunk)
        columns = slice(part * PART, (part + 1) * PART)

        def step(i, carry, chunk=chunk, columns=columns, fresh=j == 0):
            rows = pl.ds(pl.multiple_of(i * ROWS, ROWS), ROWS)
            value = products.product(chunk, rows)
            if not fresh:
                value += total[rows, columns]
            total[rows, columns] = value
            return carry

        lax.fori_loop(0, total.shape[0] // ROWS, step, 0)
    give = pltpu.make_async_copy(total, out, sem)
    give.start()
    give.wait()


def last_kernel(
    x0, x1, wb, wc, before, squares0, squares1, t0, t1,
    kv, other_kv, errors,
    x_space, w_space, total, squares, targets, halves, x_sem, w_sem, sems,
):
    core = lax.axis_index("grp") % 2
    tokens, width = x0.shape
    brought = []
    for i, (source, space) in enumerate(
        (
            (before, total),
            (squares0, squares.at[:tokens]),
            (squares1, squares.at[tokens:]),
            (t0, targets.at[:tokens]),
            (t1, targets.at[tokens:]),
        )
    ):
        brought.append(pltpu.make_async_copy(source, space, sems.at[i]))
        brought[-1].start()
    products = Products((3,), (x0, x1), (wb, wc), x_space, w_space, x_sem, w_sem)
    for copy in brought:
        copy.wait()
    errors[...] = jnp.zeros_like(errors)
    for chunk in range(2):
        products.wait(chunk)

    def step(i, carry):
        rows = pl.ds(pl.multiple_of(i * ROWS, ROWS), ROWS)
        mean = jnp.sum(squares[rows, :], axis=1, keepdims=True) / width
        scale = lax.rsqrt(mean + epsilon)
        for part in range(2):
            columns = slice(part * PART, (part + 1) * PART)
            exact = (total[rows, columns] + products.product(part, rows)) * scale
            halves[rows, columns] = exact.astype(jnp.bfloat16)
            error = exact - targets[rows, columns].astype(jnp.float32)
            error = error * error
            error = error[:, :LANES] + error[:, LANES:]
            errors[...] += jnp.sum(error.reshape(ROWS // 8, 8, LANES), axis=0)
        return carry

    lax.fori_loop(0, total.shape[0] // ROWS, step, 0)
    at = pl.multiple_of(core * HALF, HALF)
    copies = [
        pltpu.make_async_copy(halves.at[tokens:], other_kv, sems.at[0]),
        pltpu.make_async_copy(halves.at[:tokens], kv.at[:, pl.ds(at, HALF)], sems.at[1]),
    ]
    for copy in copies:
        copy.start()
    for copy in copies:
        copy.wait()


ANY = pl.BlockSpec(memory_space=pl.ANY)
HBM = pl.BlockSpec(memory_space=pltpu.HBM)
VMEM = pl.BlockSpec(memory_space=pltpu.VMEM)


def params(mib):
    return pltpu.CompilerParams(vmem_limit_bytes=mib << 20)


def cost(tokens, chunks):
    depth = 16 * LANES
    return pl.CostEstimate(
        flops=2 * chunks * 2 * tokens * depth * PART,
        transcendentals=0,
        bytes_accessed=chunks * (4 * tokens + 2 * PART) * depth + 16 * tokens * HALF,
    )


def shape(dims, kind):
    return jax.ShapeDtypeStruct(dims, kind)


def spaces(chunks, tokens):
    return [
        pltpu.VMEM((chunks, 2 * tokens, 16 * LANES), jnp.bfloat16),
        pltpu.VMEM((chunks, 16, PART, LANES), jnp.bfloat16),
        pltpu.VMEM((2 * tokens, HALF), jnp.float32),
    ]


def semaphores(chunks):
    return [pltpu.SemaphoreType.DMA((chunks,)), pltpu.SemaphoreType.DMA((chunks,))]


def add(arrivals, x, weights, before):
    tokens = x[0].shape[0]
    flat = [w for pair in weights for w in pair]
    operands = [*x, *flat] + ([] if before is None else [before])
    return pl.pallas_call(
        functools.partial(add_kernel, arrivals),
        in_specs=[HBM] * 2 + [ANY] * (len(operands) - 2),
        out_specs=ANY,
        out_shape=shape((2 * tokens, HALF), jnp.float32),
        scratch_shapes=spaces(len(flat), tokens)
        + semaphores(len(flat))
        + [pltpu.SemaphoreType.DMA(())],
        compiler_params=params(12 * len(flat) // 2 + 4),
        cost_estimate=cost(tokens, len(flat)),
    )(*operands)


def finish(x, weights, before, squares, targets):
    tokens = x[0].shape[0]
    return pl.pallas_call(
        last_kernel,
        in_specs=[HBM] * 2 + [ANY] * 7,
        out_specs=[ANY, ANY, VMEM],
        out_shape=[
            shape((tokens, 2 * HALF), jnp.bfloat16),
            shape((tokens, HALF), jnp.bfloat16),
            shape((8, LANES), jnp.float32),
        ],
        scratch_shapes=spaces(2, tokens)
        + [
            pltpu.VMEM((2 * tokens, LANES), jnp.float32),
            pltpu.VMEM((2 * tokens, HALF), jnp.bfloat16),
            pltpu.VMEM((2 * tokens, HALF), jnp.bfloat16),
        ]
        + semaphores(2)
        + [pltpu.SemaphoreType.DMA((5,))],
        compiler_params=params(24),
        cost_estimate=cost(tokens, 2),
    )(*x, *weights, before, *squares, *targets)


def sum_over(value, groups):
    length = len(groups[0])
    everything = lax.all_to_all(
        jnp.broadcast_to(value[None], (length,)), AXES, 0, 0, axis_index_groups=groups, tiled=True
    )
    return jnp.sum(everything)


def per_device(
    layer_input_rows,
    input_norm_gain,
    key_value_codes,
    block_scale_codes,
    outer_scale_codes,
    adapter_down_factor,
    adapter_up_factor,
    target,
):
    core = lax.axis_index("grp") % 2
    shard = lax.axis_index("fsdp")

    tokens = layer_input_rows.shape[0]
    other_rows = lax.ppermute(layer_input_rows, AXES, OTHER_CORE)
    own_target = lax.dynamic_slice(target, (0, core * HALF), (tokens, HALF))
    other_target = lax.ppermute(
        lax.dynamic_slice(target, (0, (1 - core) * HALF), (tokens, HALF)), AXES, OTHER_CORE
    )

    own_weight = decode(
        jnp.stack([core, shard]),
        key_value_codes,
        block_scale_codes,
        outer_scale_codes,
        input_norm_gain,
        adapter_down_factor,
        adapter_up_factor,
    )
    along_z = ring(own_weight, ZH)
    planes = []
    for part, (middle, last) in enumerate(ORDER):
        columns = slice(part * PART, (part + 1) * PART)
        line = jnp.stack([piece[columns] for piece in along_z])
        planes.append(jnp.concatenate(ring(line, middle)))

    behind = [lax.ppermute(p, AXES, FORWARD[last]) for p, (_, last) in zip(planes, ORDER)]
    ahead = [lax.ppermute(p, AXES, BACKWARD[last]) for p, (_, last) in zip(planes, ORDER)]
    own_rows, other_rows, *planes = lax.optimization_barrier(
        (layer_input_rows, other_rows, *planes)
    )
    x = (own_rows, other_rows)
    total = add((0,), x, [planes], None)
    own_squares = sum_squares(own_rows)
    total, own_squares, *behind = lax.optimization_barrier((total, own_squares, *behind))
    squares = (own_squares, lax.ppermute(own_squares, AXES, OTHER_CORE))
    opposite = [lax.ppermute(p, AXES, FORWARD[last]) for p, (_, last) in zip(behind, ORDER)]
    total = add((1, 2), x, [behind, ahead], total)
    kv, other_kv, errors = finish(x, opposite, total, squares, (own_target, other_target))
    received = lax.ppermute(other_kv, AXES, OTHER_CORE)
    kv = lax.dynamic_update_slice(kv, received, (0, (1 - core) * HALF))

    loss = jnp.sum(errors) / (tokens * lax.axis_size("fsdp") * 2 * HALF)
    for groups in LOSS_GROUPS:
        loss = sum_over(loss, groups)
    return kv, loss


def solution(mesh):
    placed = (
        P(("grp", "fsdp"), None),
        P(),
        P("fsdp", None),
        P("fsdp", None),
        P("fsdp"),
        P(),
        P(),
        P(("grp", "fsdp"), None),
    )
    return jax.shard_map(
        per_device,
        mesh=mesh,
        in_specs=placed,
        out_specs=(P(("grp", "fsdp"), None), P()),
        check_vma=False,
    )
```

time: 304 us -> 131 us (0.43)
  waiting for transfers between devices: 223 us -> 12.7 us
  Pallas kernels: 0 us -> 33.7 us
  starting transfers between devices: 0.04 us -> 32.9 us
  matrix products: 24.7 us -> 0 us
  local copies, waits for them, and re-layouts: 3 us -> 20.9 us
  between operations: 14.8 us -> 1.47 us
  other arithmetic: 9.34 us -> 2.54 us
  blocking collectives: 29.2 us -> 25.6 us
    all_gather x1 -> x0, waiting for transfers between devices: 223 us -> none  [per_device(): lax.all_gather(owned, 'fsdp', axis=0, tiled=True)]
    pallas_call x0 -> x5, Pallas kernels: none -> 33.7 us  [the longest x2 16 us: add(): pl.pallas_call(functools.partial(add_kernel, arrivals), in_specs=[HBM] *...]
    ppermute x0 -> x19, starting transfers between devices: none -> 32.9 us  [the longest x3 10.1 us: ring(): opposite = lax.ppermute(behind, AXES, FORWARD[axis])]
    dot_general x2 -> x0, matrix products: 24.7 us -> none  [the longest x1 16.8 us: per_device(): jnp.dot(normed_input, lax.all_gather(owned, 'fsdp', axis=0, tiled=True),...]
    unnamed x7 -> x16, local copies, waits for them, and re-layouts: 1.01 us -> 15.1 us
    ppermute x0 -> x19, waiting for transfers between devices: none -> 12.7 us  [the longest x3 6.29 us: ring(): behind = lax.ppermute(block, AXES, FORWARD[axis])]
    reduce_sum x3, other arithmetic: 6.37 us -> 1.83 us  [the longest x2 1.23 us: sum_over(): return jnp.sum(everything)]
    all_to_all x2, blocking collectives: 29.2 us -> 25.6 us  [sum_over(): lax.all_to_all(jnp.broadcast_to(value[None], (length,)), AXES, 0, 0, axis...]
  transfers between devices with their start and end apart: 1 -> 19, of which waited for: 1 -> 7; matrix products, arithmetic and copies ran while one was open for 5% -> 10% of each run, Pallas kernels for 0% -> 20%
where the time goes in v1:
time: 131 us; the launch traced here: 130 us
  Pallas kernels  33.7 us (26%)
  starting transfers between devices  32.9 us (25%)
  blocking collectives  25.6 us (20%)
  local copies, waits for them, and re-layouts  20.9 us (16%)
  waiting for transfers between devices  12.7 us (10%)
  other arithmetic  2.54 us (2%)
  between operations  1.47 us (1%)
    all_to_all x2, blocking collectives, sum_over(): lax.all_to_all(jnp.broadcast_to(value[None], (length,)), AXES, 0, 0, axis...  25.6 us
    pallas_call x2, Pallas kernels, add(): pl.pallas_call(functools.partial(add_kernel, arrivals), in_specs=[HBM] *...  16 us
    unnamed x16, local copies, waits for them, and re-layouts  15.1 us
    ppermute x3, starting transfers between devices, ring(): opposite = lax.ppermute(behind, AXES, FORWARD[axis])  10.1 us
    ppermute x4, starting transfers between devices, per_device(): lax.ppermute(p, AXES, FORWARD[last])  9.37 us
    ppermute x3, starting transfers between devices, ring(): behind = lax.ppermute(block, AXES, FORWARD[axis])  9.31 us
    pallas_call x1, Pallas kernels, sum_squares(): pl.pallas_call(squares_kernel, grid=(8,), in_specs=[pl.BlockSpec((tokens...  7.7 us
    pallas_call x1, Pallas kernels, finish(): pl.pallas_call(last_kernel, in_specs=[HBM] * 2 + [ANY] * 7, out_specs=[AN...  7.3 us
  transfers between devices with their start and end apart: 19, of which 7 were waited for; matrix products, arithmetic and copies ran while one was open for 10% of the time, Pallas kernels for 20%

profile of v1, /device:TPU:1, one launch (start us, length us, event | category | flops | bytes accessed | tf_op | source)
XLA Modules:
  0.0 129.8 jit_solution(11475517399979978700)
XLA Ops:
  0.6 3.3 %collective-permute-start = (bf16[512,8192]{1,0:T(8,128)(2,1)}, bf16[512,8192]{1,0:T(8,128)(2,1)}, u32[]{:S(2)}, u32[]{:S(2)}) collective-permute-start(bf16[512,8192]{1,0:T(8,128)(2,1)} %x0), channel_id=1, source_target_pairs={{0,64},{1,65},{2,66},{3,67},{4,68},{5,69},{6,70},{7,71},{8,72},{9,... | collective-permute-start | bytes 25165832 | tf_op jit(solution)/shard_map/ppermute | solution.py:422
  4.0 1.4 %copy.12.gain = bf16[64,1,128]{2,1,0:T(2,128)(2,1)} copy(bf16[64,1,128]{2,0,1:T(8,128)(2,1)} %bitcast.37) | data formatting | bytes 32768 | tf_op jit(solution)/shard_map/reshape | solution.py:142
  5.3 0.6 pad_add_fusion.place
  5.9 2.7 %shard_map.95 = bf16[512,128]{1,0:T(8,128)(2,1)} custom-call(s32[2]{0:T(128)} %pad_add_fusion.place, s32[8]{0:T(128)} %outer.1, s32[128,256]{1,0:T(8,128)} %words.1, s32[4,128]{1,0:T(4,128)} %scale_words.1, bf16[64,1,128]{2,1,0:T(2,128)(2,1)} %copy.12.gain, bf16[64,8192]{1,0:T(8,128)(2,1)} %bitcast.36, bf16[64,1024]{1,0:T(8,128)(2,1)} %up.1), custom_call_target="tpu_custom_call" | custom-call | tf_op jit(solution)/shard_map/pallas_call | solution.py:138
  8.7 4.3 %collective-permute-start.1 = (bf16[512,128]{1,0:T(8,128)(2,1)}, bf16[512,128]{1,0:T(8,128)(2,1)S(1)}, u32[]{:S(2)}, u32[]{:S(2)}) collective-permute-start(bf16[512,128]{1,0:T(8,128)(2,1)} %shard_map.95), channel_id=1, source_target_pairs={{0,16},{1,17},{2,18},{3,19},{4,20},{5,21},{6,22},{7,23},{8,24},{9,... | collective-permute-start | bytes 393224 | tf_op jit(solution)/shard_map/ppermute | solution.py:66
  13.0 1.5 %constant_dynamic-update-slice_fusion.13 = (bf16[16,256,128]{2,1,0:T(8,128)(2,1)S(1)}, bf16[16,256,128]{2,1,0:T(8,128)(2,1)}) fusion(bf16[512,128]{1,0:T(8,128)(2,1)} %shard_map.95), kind=kLoop, calls=%fused_computation.23 | loop fusion | bytes 262144
  14.5 0.9 slice_bitcast_fusion.3
  15.4 3.4 %collective-permute-done.1 = bf16[512,128]{1,0:T(8,128)(2,1)S(1)} collective-permute-done((bf16[512,128]{1,0:T(8,128)(2,1)}, bf16[512,128]{1,0:T(8,128)(2,1)S(1)}, u32[]{:S(2)}, u32[]{:S(2)}) %collective-permute-start.1) | collective-permute-done | bytes 131104 | tf_op jit(solution)/shard_map/ppermute | solution.py:66
  18.8 4.3 %collective-permute-start.3 = (bf16[512,128]{1,0:T(8,128)(2,1)S(1)}, bf16[512,128]{1,0:T(8,128)(2,1)S(1)}, u32[]{:S(2)}, u32[]{:S(2)}) collective-permute-start(bf16[512,128]{1,0:T(8,128)(2,1)S(1)} %collective-permute-done.1), channel_id=1, source_target_pairs={{0,16},{1,17},{2,18},{3,19},{4,20},{5,21},{6,22},{7,23},{8,24},{9,... | collective-permute-start | bytes 393224 | tf_op jit(solution)/shard_map/ppermute | solution.py:68
  23.2 0.6 constant_dynamic-update-slice_fusion.12
  23.9 0.6 constant_dynamic-update-slice_fusion.11
  24.5 1.9 %collective-permute-done.3 = bf16[512,128]{1,0:T(8,128)(2,1)S(1)} collective-permute-done((bf16[512,128]{1,0:T(8,128)(2,1)S(1)}, bf16[512,128]{1,0:T(8,128)(2,1)S(1)}, u32[]{:S(2)}, u32[]{:S(2)}) %collective-permute-start.3) | collective-permute-done | bytes 131104 | tf_op jit(solution)/shard_map/ppermute | solution.py:68
  26.5 2.1 %collective-permute-start.7 = (bf16[4,256,128]{2,1,0:T(8,128)(2,1)S(1)}, bf16[4,256,128]{2,1,0:T(8,128)(2,1)S(1)}, u32[]{:S(2)}, u32[]{:S(2)}) collective-permute-start(bf16[4,256,128]{2,1,0:T(8,128)(2,1)S(1)} %pad_maximum_fusion.1), channel_id=1, source_target_pairs={{0,4},{1,5},{2,6},{3,7},{4,8},{5,9},{6,10},{7,11},{8,12},{9,13},{1... | collective-permute-start | bytes 786440 | tf_op jit(solution)/shard_map/ppermute | solution.py:66
  28.7 2.9 %collective-permute-start.4 = (bf16[4,256,128]{2,1,0:T(8,128)(2,1)S(1)}, bf16[4,256,128]{2,1,0:T(8,128)(2,1)S(1)}, u32[]{:S(2)}, u32[]{:S(2)}) collective-permute-start(bf16[4,256,128]{2,1,0:T(8,128)(2,1)S(1)} %pad_maximum_fusion), channel_id=1, source_target_pairs={{0,1},{1,2},{2,3},{3,0},{4,5},{5,6},{6,7},{7,4},{8,9},{9,10},{10,1... | collective-permute-start | bytes 786440 | tf_op jit(solution)/shard_map/ppermute | solution.py:66
  31.6 0.6 constant_dynamic-update-slice_fusion.10
  32.2 2.6 %collective-permute-done.7 = bf16[4,256,128]{2,1,0:T(8,128)(2,1)S(1)} collective-permute-done((bf16[4,256,128]{2,1,0:T(8,128)(2,1)S(1)}, bf16[4,256,128]{2,1,0:T(8,128)(2,1)S(1)}, u32[]{:S(2)}, u32[]{:S(2)}) %collective-permute-start.7) | collective-permute-done | bytes 262176 | tf_op jit(solution)/shard_map/ppermute | solution.py:66
  34.9 2.4 %collective-permute-start.9 = (bf16[4,256,128]{2,1,0:T(8,128)(2,1)S(1)}, bf16[4,256,128]{2,1,0:T(8,128)(2,1)S(1)}, u32[]{:S(2)}, u32[]{:S(2)}) collective-permute-start(bf16[4,256,128]{2,1,0:T(8,128)(2,1)S(1)} %collective-permute-done.7), channel_id=1, source_target_pairs={{0,4},{1,5},{2,6},{3,7},{4,8},{5,9},{6,10},{7,11},{8,12},{9,13},{1... | collective-permute-start | bytes 786440 | tf_op jit(solution)/shard_map/ppermute | solution.py:68
  37.3 0.2 collective-permute-done.4
  37.5 3.4 %collective-permute-start.6 = (bf16[4,256,128]{2,1,0:T(8,128)(2,1)S(1)}, bf16[4,256,128]{2,1,0:T(8,128)(2,1)S(1)}, u32[]{:S(2)}, u32[]{:S(2)}) collective-permute-start(bf16[4,256,128]{2,1,0:T(8,128)(2,1)S(1)} %collective-permute-done.4), channel_id=1, source_target_pairs={{0,1},{1,2},{2,3},{3,0},{4,5},{5,6},{6,7},{7,4},{8,9},{9,10},{10,1... | collective-permute-start | bytes 786440 | tf_op jit(solution)/shard_map/ppermute | solution.py:68
  40.9 0.7 constant_dynamic-update-slice_fusion.2
  41.7 0.7 constant_dynamic-update-slice_fusion.1
  42.4 1.3 collective-permute-start.11
  43.7 0.5 collective-permute-done.6
  44.2 0.7 constant_dynamic-update-slice_fusion.refs_2_
  44.9 2.6 %collective-permute-start.10 = (bf16[16,256,128]{2,1,0:T(8,128)(2,1)}, bf16[16,256,128]{2,1,0:T(8,128)(2,1)}, u32[]{:S(2)}, u32[]{:S(2)}) collective-permute-start(bf16[16,256,128]{2,1,0:T(8,128)(2,1)} %constant_dynamic-update-slice_fusion.refs_2_), channel_id=1, source_target_pairs={{0,4},{1,5},{2,6},{3,7},{4,8},{5,9},{6,10},{7,11},{8,12},{9,13},{1... | collective-permute-start | bytes 3145736 | tf_op jit(solution)/shard_map/ppermute | solution.py:444
  47.6 7.7 %shard_map.97.squares0 = f32[512,128]{1,0:T(8,128)} custom-call(bf16[512,8192]{1,0:T(8,128)(2,1)} %x0), custom_call_target="tpu_custom_call" | custom-call | flops 8388608 | bytes 8388608 | tf_op jit(solution)/shard_map/pallas_call | solution.py:165
  55.3 3.4 %copy-done = bf16[512,8192]{1,0:T(8,128)(2,1)S(1)} copy-done((bf16[512,8192]{1,0:T(8,128)(2,1)S(1)}, bf16[512,8192]{1,0:T(8,128)(2,1)}, u32[]{:S(2)}) %copy-start) | copy-done | bytes 8388632
  58.6 5.9 %shard_map.96.refs_6_ = f32[1024,512]{1,0:T(8,128)S(1)} custom-call(bf16[512,8192]{1,0:T(8,128)(2,1)S(1)} %copy-done, bf16[512,8192]{1,0:T(8,128)(2,1)} %collective-permute-done.refs_1_.x1, bf16[16,256,128]{2,1,0:T(8,128)(2,1)} %constant_dynamic-update-slice_fusion.refs_2_, bf16[16,256,128]{2,1,0:T(8,128)(2,1)S(1)} %constant_dynamic-update-slice_fusion.7.refs_3_), custom_call_target="tpu_custom_call" | custom-call | flops 2147483648 | bytes 14680064 | tf_op jit(solution)/shard_map/pallas_call | solution.py:363
  64.6 0.8 collective-permute-done.11.refs_3_
  65.4 3.2 %collective-permute-done.10.refs_2_ = bf16[16,256,128]{2,1,0:T(8,128)(2,1)} collective-permute-done((bf16[16,256,128]{2,1,0:T(8,128)(2,1)}, bf16[16,256,128]{2,1,0:T(8,128)(2,1)}, u32[]{:S(2)}, u32[]{:S(2)}) %collective-permute-start.10) | collective-permute-done | bytes 1048608 | tf_op jit(solution)/shard_map/ppermute | solution.py:444
  68.6 3.4 %collective-permute-start.12 = (bf16[16,256,128]{2,1,0:T(8,128)(2,1)}, bf16[16,256,128]{2,1,0:T(8,128)(2,1)}, u32[]{:S(2)}, u32[]{:S(2)}) collective-permute-start(bf16[16,256,128]{2,1,0:T(8,128)(2,1)} %collective-permute-done.10.refs_2_), channel_id=1, source_target_pairs={{0,4},{1,5},{2,6},{3,7},{4,8},{5,9},{6,10},{7,11},{8,12},{9,13},{1... | collective-permute-start | bytes 3145736 | tf_op jit(solution)/shard_map/ppermute | solution.py:454
  72.0 2.1 %collective-permute-start.13 = (bf16[16,256,128]{2,1,0:T(8,128)(2,1)}, bf16[16,256,128]{2,1,0:T(8,128)(2,1)}, u32[]{:S(2)}, u32[]{:S(2)}) collective-permute-start(bf16[16,256,128]{2,1,0:T(8,128)(2,1)} %collective-permute-done.11.refs_3_), channel_id=1, source_target_pairs={{0,1},{1,2},{2,3},{3,0},{4,5},{5,6},{6,7},{7,4},{8,9},{9,10},{10,1... | collective-permute-start | bytes 3145736 | tf_op jit(solution)/shard_map/ppermute | solution.py:454
  74.0 1.3 constant_dynamic-slice_fusion
  75.3 0.1 collective-permute-start.17
  75.4 0.5 collective-permute-start.16
  75.9 3.4 %copy-done.1 = bf16[512,8192]{1,0:T(8,128)(2,1)S(1)} copy-done((bf16[512,8192]{1,0:T(8,128)(2,1)S(1)}, bf16[512,8192]{1,0:T(8,128)(2,1)}, u32[]{:S(2)}) %copy-start.1) | copy-done | bytes 8388632
  79.3 10.0 %shard_map.98.before = f32[1024,512]{1,0:T(8,128)S(1)} custom-call(bf16[512,8192]{1,0:T(8,128)(2,1)S(1)} %copy-done.1, bf16[512,8192]{1,0:T(8,128)(2,1)} %collective-permute-done.refs_1_.x1, bf16[16,256,128]{2,1,0:T(8,128)(2,1)} %collective-permute-done.10.refs_2_, bf16[16,256,128]{2,1,0:T(8,128)(2,1)} %collective-permute-done.11.refs_3_, ...), custom_call_target="tpu_custom_call" | custom-call | flops 4294967296 | bytes 25165824 | tf_op jit(solution)/shard_map/pallas_call | solution.py:363
  89.4 0.0 copy-start.2
  89.4 3.4 %copy-done.2 = bf16[512,8192]{1,0:T(8,128)(2,1)S(1)} copy-done((bf16[512,8192]{1,0:T(8,128)(2,1)S(1)}, bf16[512,8192]{1,0:T(8,128)(2,1)}, u32[]{:S(2)}) %copy-start.2) | copy-done | bytes 8388632
  92.8 7.3 %shard_map.99 = (bf16[512,1024]{1,0:T(8,128)(2,1)}, bf16[512,512]{1,0:T(8,128)(2,1)S(1)}, f32[8,128]{1,0:T(8,128)S(1)}) custom-call(bf16[512,8192]{1,0:T(8,128)(2,1)S(1)} %copy-done.2, bf16[512,8192]{1,0:T(8,128)(2,1)} %collective-permute-done.refs_1_.x1, bf16[16,256,128]{2,1,0:T(8,128)(2,1)} %collective-permute-done.12.wb, ...), custom_call_target="tpu_custom_call" | custom-call | flops 2147483648 | bytes 14680064 | tf_op jit(solution)/shard_map/pallas_call | solution.py:378
  100.1 0.2 collective-permute-start.18
  100.3 0.6 reduce_sum.27
  101.5 9.0 %all_to_all.12 = f32[16,1,1]{2,1,0:T(1,128)S(1)} all-to-all(f32[16,1,1]{2,1,0:T(1,128)S(1)} %broadcast_in_dim.4), channel_id=1, replica_groups={{0,1,2,3,4,5,6,7,8,9,10,11,12,13,14,15},{16,17,18,19,20,21,22,23,24,25,..., dimensions={0} | all-to-all | bytes 128 | tf_op jit(solution)/shard_map/all_to_all | solution.py:402
  110.5 0.6 reduce_sum.28
  111.1 0.6 broadcast_in_dim.5
  111.8 16.6 %all_to_all.13 = f32[16,1,1]{2,1,0:T(1,128)S(1)} all-to-all(f32[16,1,1]{2,1,0:T(1,128)S(1)} %broadcast_in_dim.5), channel_id=1, replica_groups={{0,16,32,48,64,80,96,112,128,144,160,176,192,208,224,240},{1,17,33,49,6..., dimensions={0} | all-to-all | bytes 128 | tf_op jit(solution)/shard_map/all_to_all | solution.py:402
  128.4 0.6 reduce_sum.29
  129.0 0.8 constant_dynamic-update-slice_fusion.14
  (30 shorter events, 0.3 us)
Async XLA Ops:
  0.6 46.9 %collective-permute-start = (bf16[512,8192]{1,0:T(8,128)(2,1)}, bf16[512,8192]{1,0:T(8,128)(2,1)}, u32[]{:S(2)}, u32[]{:S(2)}) collective-permute-start(bf16[512,8192]{1,0:T(8,128)(2,1)} %x0), channel_id=1, source_target_pairs={{0,64},{1,65},{2,66},{3,67},{4,68},{5,69},{6,70},{7,71},{8,72},{9,... | collective-permute-start | bytes 25165832 | tf_op jit(solution)/shard_map/ppermute | solution.py:422
  8.7 10.2 %collective-permute-start.1 = (bf16[512,128]{1,0:T(8,128)(2,1)}, bf16[512,128]{1,0:T(8,128)(2,1)S(1)}, u32[]{:S(2)}, u32[]{:S(2)}) collective-permute-start(bf16[512,128]{1,0:T(8,128)(2,1)} %shard_map.95), channel_id=1, source_target_pairs={{0,16},{1,17},{2,18},{3,19},{4,20},{5,21},{6,22},{7,23},{8,24},{9,... | collective-permute-start | bytes 393224 | tf_op jit(solution)/shard_map/ppermute | solution.py:66
  13.0 10.2 %collective-permute-start.2 = (bf16[512,128]{1,0:T(8,128)(2,1)}, bf16[512,128]{1,0:T(8,128)(2,1)S(1)}, u32[]{:S(2)}, u32[]{:S(2)}) collective-permute-start(bf16[512,128]{1,0:T(8,128)(2,1)} %shard_map.95), channel_id=1, source_target_pairs={{0,48},{1,49},{2,50},{3,51},{4,52},{5,53},{6,54},{7,55},{8,56},{9,... | collective-permute-start | bytes 393224 | tf_op jit(solution)/shard_map/ppermute | solution.py:67
  18.8 7.6 %collective-permute-start.3 = (bf16[512,128]{1,0:T(8,128)(2,1)S(1)}, bf16[512,128]{1,0:T(8,128)(2,1)S(1)}, u32[]{:S(2)}, u32[]{:S(2)}) collective-permute-start(bf16[512,128]{1,0:T(8,128)(2,1)S(1)} %collective-permute-done.1), channel_id=1, source_target_pairs={{0,16},{1,17},{2,18},{3,19},{4,20},{5,21},{6,22},{7,23},{8,24},{9,... | collective-permute-start | bytes 393224 | tf_op jit(solution)/shard_map/ppermute | solution.py:68
  26.5 8.4 %collective-permute-start.7 = (bf16[4,256,128]{2,1,0:T(8,128)(2,1)S(1)}, bf16[4,256,128]{2,1,0:T(8,128)(2,1)S(1)}, u32[]{:S(2)}, u32[]{:S(2)}) collective-permute-start(bf16[4,256,128]{2,1,0:T(8,128)(2,1)S(1)} %pad_maximum_fusion.1), channel_id=1, source_target_pairs={{0,4},{1,5},{2,6},{3,7},{4,8},{5,9},{6,10},{7,11},{8,12},{9,13},{1... | collective-permute-start | bytes 786440 | tf_op jit(solution)/shard_map/ppermute | solution.py:66
  28.6 13.0 %collective-permute-start.8 = (bf16[4,256,128]{2,1,0:T(8,128)(2,1)S(1)}, bf16[4,256,128]{2,1,0:T(8,128)(2,1)S(1)}, u32[]{:S(2)}, u32[]{:S(2)}) collective-permute-start(bf16[4,256,128]{2,1,0:T(8,128)(2,1)S(1)} %pad_maximum_fusion.1), channel_id=1, source_target_pairs={{0,12},{1,13},{2,14},{3,15},{4,0},{5,1},{6,2},{7,3},{8,4},{9,5},{1... | collective-permute-start | bytes 786440 | tf_op jit(solution)/shard_map/ppermute | solution.py:67
  28.7 8.8 %collective-permute-start.4 = (bf16[4,256,128]{2,1,0:T(8,128)(2,1)S(1)}, bf16[4,256,128]{2,1,0:T(8,128)(2,1)S(1)}, u32[]{:S(2)}, u32[]{:S(2)}) collective-permute-start(bf16[4,256,128]{2,1,0:T(8,128)(2,1)S(1)} %pad_maximum_fusion), channel_id=1, source_target_pairs={{0,1},{1,2},{2,3},{3,0},{4,5},{5,6},{6,7},{7,4},{8,9},{9,10},{10,1... | collective-permute-start | bytes 786440 | tf_op jit(solution)/shard_map/ppermute | solution.py:66
  31.6 10.1 %collective-permute-start.5 = (bf16[4,256,128]{2,1,0:T(8,128)(2,1)S(1)}, bf16[4,256,128]{2,1,0:T(8,128)(2,1)S(1)}, u32[]{:S(2)}, u32[]{:S(2)}) collective-permute-start(bf16[4,256,128]{2,1,0:T(8,128)(2,1)S(1)} %pad_maximum_fusion), channel_id=1, source_target_pairs={{0,3},{1,0},{2,1},{3,2},{4,7},{5,4},{6,5},{7,6},{8,11},{9,8},{10,9... | collective-permute-start | bytes 786440 | tf_op jit(solution)/shard_map/ppermute | solution.py:67
  34.9 7.5 %collective-permute-start.9 = (bf16[4,256,128]{2,1,0:T(8,128)(2,1)S(1)}, bf16[4,256,128]{2,1,0:T(8,128)(2,1)S(1)}, u32[]{:S(2)}, u32[]{:S(2)}) collective-permute-start(bf16[4,256,128]{2,1,0:T(8,128)(2,1)S(1)} %collective-permute-done.7), channel_id=1, source_target_pairs={{0,4},{1,5},{2,6},{3,7},{4,8},{5,9},{6,10},{7,11},{8,12},{9,13},{1... | collective-permute-start | bytes 786440 | tf_op jit(solution)/shard_map/ppermute | solution.py:68
  37.5 6.7 %collective-permute-start.6 = (bf16[4,256,128]{2,1,0:T(8,128)(2,1)S(1)}, bf16[4,256,128]{2,1,0:T(8,128)(2,1)S(1)}, u32[]{:S(2)}, u32[]{:S(2)}) collective-permute-start(bf16[4,256,128]{2,1,0:T(8,128)(2,1)S(1)} %collective-permute-done.4), channel_id=1, source_target_pairs={{0,1},{1,2},{2,3},{3,0},{4,5},{5,6},{6,7},{7,4},{8,9},{9,10},{10,1... | collective-permute-start | bytes 786440 | tf_op jit(solution)/shard_map/ppermute | solution.py:68
  42.4 23.0 %collective-permute-start.11 = (bf16[16,256,128]{2,1,0:T(8,128)(2,1)S(1)}, bf16[16,256,128]{2,1,0:T(8,128)(2,1)}, u32[]{:S(2)}, u32[]{:S(2)}) collective-permute-start(bf16[16,256,128]{2,1,0:T(8,128)(2,1)S(1)} %constant_dynamic-update-slice_fusion.7.refs_3_), channel_id=1, source_target_pairs={{0,1},{1,2},{2,3},{3,0},{4,5},{5,6},{6,7},{7,4},{8,9},{9,10},{10,1... | collective-permute-start | bytes 3145736 | tf_op jit(solution)/shard_map/ppermute | solution.py:444
  44.9 23.6 %collective-permute-start.10 = (bf16[16,256,128]{2,1,0:T(8,128)(2,1)}, bf16[16,256,128]{2,1,0:T(8,128)(2,1)}, u32[]{:S(2)}, u32[]{:S(2)}) collective-permute-start(bf16[16,256,128]{2,1,0:T(8,128)(2,1)} %constant_dynamic-update-slice_fusion.refs_2_), channel_id=1, source_target_pairs={{0,4},{1,5},{2,6},{3,7},{4,8},{5,9},{6,10},{7,11},{8,12},{9,13},{1... | collective-permute-start | bytes 3145736 | tf_op jit(solution)/shard_map/ppermute | solution.py:444
  47.6 27.9 %collective-permute-start.15 = (bf16[16,256,128]{2,1,0:T(8,128)(2,1)S(1)}, bf16[16,256,128]{2,1,0:T(8,128)(2,1)}, u32[]{:S(2)}, u32[]{:S(2)}) collective-permute-start(bf16[16,256,128]{2,1,0:T(8,128)(2,1)S(1)} %constant_dynamic-update-slice_fusion.7.refs_3_), channel_id=1, source_target_pairs={{0,3},{1,0},{2,1},{3,2},{4,7},{5,4},{6,5},{7,6},{8,11},{9,8},{10,9... | collective-permute-start | bytes 3145736 | tf_op jit(solution)/shard_map/ppermute | solution.py:445
  47.6 28.4 %collective-permute-start.14 = (bf16[16,256,128]{2,1,0:T(8,128)(2,1)}, bf16[16,256,128]{2,1,0:T(8,128)(2,1)}, u32[]{:S(2)}, u32[]{:S(2)}) collective-permute-start(bf16[16,256,128]{2,1,0:T(8,128)(2,1)} %constant_dynamic-update-slice_fusion.refs_2_), channel_id=1, source_target_pairs={{0,12},{1,13},{2,14},{3,15},{4,0},{5,1},{6,2},{7,3},{8,4},{9,5},{1... | collective-permute-start | bytes 3145736 | tf_op jit(solution)/shard_map/ppermute | solution.py:445
  55.3 3.4 %copy-start = (bf16[512,8192]{1,0:T(8,128)(2,1)S(1)}, bf16[512,8192]{1,0:T(8,128)(2,1)}, u32[]{:S(2)}) copy-start(bf16[512,8192]{1,0:T(8,128)(2,1)} %x0) | copy-start | bytes 25165828
  58.6 16.8 %copy-start.3 = (f32[512,128]{1,0:T(8,128)S(1)}, f32[512,128]{1,0:T(8,128)}, u32[]{:S(2)}) copy-start(f32[512,128]{1,0:T(8,128)} %shard_map.97.squares0) | copy-start | bytes 786436
  68.6 20.8 %collective-permute-start.12 = (bf16[16,256,128]{2,1,0:T(8,128)(2,1)}, bf16[16,256,128]{2,1,0:T(8,128)(2,1)}, u32[]{:S(2)}, u32[]{:S(2)}) collective-permute-start(bf16[16,256,128]{2,1,0:T(8,128)(2,1)} %collective-permute-done.10.refs_2_), channel_id=1, source_target_pairs={{0,4},{1,5},{2,6},{3,7},{4,8},{5,9},{6,10},{7,11},{8,12},{9,13},{1... | collective-permute-start | bytes 3145736 | tf_op jit(solution)/shard_map/ppermute | solution.py:454
  72.0 17.4 %collective-permute-start.13 = (bf16[16,256,128]{2,1,0:T(8,128)(2,1)}, bf16[16,256,128]{2,1,0:T(8,128)(2,1)}, u32[]{:S(2)}, u32[]{:S(2)}) collective-permute-start(bf16[16,256,128]{2,1,0:T(8,128)(2,1)} %collective-permute-done.11.refs_3_), channel_id=1, source_target_pairs={{0,1},{1,2},{2,3},{3,0},{4,5},{5,6},{6,7},{7,4},{8,9},{9,10},{10,1... | collective-permute-start | bytes 3145736 | tf_op jit(solution)/shard_map/ppermute | solution.py:454
  75.3 14.0 %collective-permute-start.17 = (bf16[512,512]{1,0:T(8,128)(2,1)S(1)}, bf16[512,512]{1,0:T(8,128)(2,1)S(1)}, u32[]{:S(2)}, u32[]{:S(2)}) collective-permute-start(bf16[512,512]{1,0:T(8,128)(2,1)S(1)} %get-tuple-element.24), channel_id=1, source_target_pairs={{0,64},{1,65},{2,66},{3,67},{4,68},{5,69},{6,70},{7,71},{8,72},{9,... | collective-permute-start | bytes 1572872 | tf_op jit(solution)/shard_map/ppermute | solution.py:424
  75.4 13.9 %collective-permute-start.16 = (f32[512,128]{1,0:T(8,128)S(1)}, f32[512,128]{1,0:T(8,128)S(1)}, u32[]{:S(2)}, u32[]{:S(2)}) collective-permute-start(f32[512,128]{1,0:T(8,128)S(1)} %copy-done.3), channel_id=1, source_target_pairs={{0,64},{1,65},{2,66},{3,67},{4,68},{5,69},{6,70},{7,71},{8,72},{9,... | collective-permute-start | bytes 786440 | tf_op jit(solution)/shard_map/ppermute | solution.py:453
  75.9 3.4 %copy-start.1 = (bf16[512,8192]{1,0:T(8,128)(2,1)S(1)}, bf16[512,8192]{1,0:T(8,128)(2,1)}, u32[]{:S(2)}) copy-start(bf16[512,8192]{1,0:T(8,128)(2,1)} %x0) | copy-start | bytes 25165828
  89.4 3.4 %copy-start.2 = (bf16[512,8192]{1,0:T(8,128)(2,1)S(1)}, bf16[512,8192]{1,0:T(8,128)(2,1)}, u32[]{:S(2)}) copy-start(bf16[512,8192]{1,0:T(8,128)(2,1)} %x0) | copy-start | bytes 25165828
  100.1 28.9 %collective-permute-start.18 = (bf16[512,512]{1,0:T(8,128)(2,1)S(1)}, bf16[512,512]{1,0:T(8,128)(2,1)S(1)}, u32[]{:S(2)}, u32[]{:S(2)}) collective-permute-start(bf16[512,512]{1,0:T(8,128)(2,1)S(1)} %get-tuple-element.22), channel_id=1, source_target_pairs={{0,64},{1,65},{2,66},{3,67},{4,68},{5,69},{6,70},{7,71},{8,72},{9,... | collective-permute-start | bytes 1572872 | tf_op jit(solution)/shard_map/ppermute | solution.py:457

commit v2 on v0

v2 whole, which is shorter than its diff:
```python
import functools

import numpy as np

import jax
import jax.numpy as jnp
from jax import lax
from jax.experimental import pallas as pl
from jax.experimental.pallas import tpu as pltpu
from jax.sharding import PartitionSpec as P

adapter_scale = 0.25
epsilon = 1e-06
nf4_levels = (
    -1.0,
    -0.6961928009986877,
    -0.5250730514526367,
    -0.39491748809814453,
    -0.28444138169288635,
    -0.18477343022823334,
    -0.09105003625154495,
    0.0,
    0.07958029955625534,
    0.16093020141124725,
    0.24611230194568634,
    0.33791524171066284,
    0.44070982933044434,
    0.5626170039176941,
    0.7229568362236023,
    1.0,
)

AXES = ("grp", "fsdp")
LANES = 128
PART = 256
HALF = 2 * PART


def permutation(move):
    sizes = (2, 2, 4, 4, 4)
    pairs = []
    for source in range(int(np.prod(sizes))):
        place = [int(v) for v in np.unravel_index(source, sizes)]
        target = [v % s for v, s in zip(move(*place), sizes)]
        pairs.append((source, int(np.ravel_multi_index(target, sizes))))
    return pairs


def along(axis, step):
    def move(*place):
        place = list(place)
        place[axis] += step if place[1] == 0 else -step
        return place

    return permutation(move)


ZH, X, Y = 2, 3, 4
FORWARD = {axis: along(axis, 1) for axis in (ZH, X, Y)}
BACKWARD = {axis: along(axis, -1) for axis in (ZH, X, Y)}
ORDER = ((Y, X), (X, Y))
STRIDE = {ZH: 16, X: 4, Y: 1}
ACROSS_ZH = permutation(lambda zl, c, zh, x, y: (1 - zl, c, zh + 2, x, y))
OTHER_CORE = permutation(lambda zl, c, zh, x, y: (zl, 1 - c, zh, x, y))


def ring(block, axis):
    behind = lax.ppermute(block, AXES, FORWARD[axis])
    ahead = lax.ppermute(block, AXES, BACKWARD[axis])
    if axis == ZH:
        opposite = lax.ppermute(block, AXES, ACROSS_ZH)
    else:
        opposite = lax.ppermute(behind, AXES, FORWARD[axis])
    return [block, behind, ahead, opposite]


_DEVICES = np.arange(256).reshape(2, 2, 4, 16).transpose(0, 2, 1, 3).reshape(8, 32)
LOSS_GROUPS = (_DEVICES.tolist(), _DEVICES.T.tolist())


ANY = pl.BlockSpec(memory_space=pl.ANY)
VMEM = pl.BlockSpec(memory_space=pltpu.VMEM)
SMEM = pl.BlockSpec(memory_space=pltpu.SMEM)


def shape(dims, kind):
    return jax.ShapeDtypeStruct(dims, kind)


def params(mib):
    return pltpu.CompilerParams(vmem_limit_bytes=mib << 20)


def decode_kernel(
    outer, words, scale_words, gain, down, up, whole, levels, own_words, own_down, own_up, sems
):
    core = lax.axis_index("grp") % 2
    shard = lax.axis_index("fsdp")
    lanes = pl.ds(pl.multiple_of(core * LANES, LANES), LANES)
    rows = pl.ds(pl.multiple_of(shard * LANES, LANES), LANES)
    half = pl.ds(pl.multiple_of(core * HALF, HALF), HALF)
    copies = [
        pltpu.make_async_copy(words.at[:, lanes], own_words, sems.at[0]),
        pltpu.make_async_copy(down.at[:, rows], own_down, sems.at[1]),
        pltpu.make_async_copy(up.at[:, half], own_up, sems.at[2]),
    ]
    for copy in copies:
        copy.start()
    for copy in copies:
        copy.wait()
    words_t = jnp.transpose(own_words[...])
    for j in range(4):
        code = jnp.bitwise_and(jnp.right_shift(words_t, 4 * j), 15)
        value = jnp.full(code.shape, nf4_levels[0], jnp.float32)
        for number in range(1, 16):
            value = jnp.where(code == number, jnp.float32(nf4_levels[number]), value)
        levels[pl.ds(j, LANES, stride=4), :] = value
    row = lax.broadcasted_iota(jnp.int32, (1, LANES), 1)
    second = jnp.zeros((1, LANES), jnp.float32)
    for g in range(8):
        code = outer[g].astype(jnp.float32)
        second = jnp.where(row // 16 == g, code, second)
    second = jnp.exp2(second / 128.0 - 6.0)
    code_bytes = jnp.concatenate(
        [
            jnp.bitwise_and(jnp.right_shift(scale_words[...], 8 * j), 255).astype(jnp.float32)
            for j in range(4)
        ],
        axis=0,
    ).astype(jnp.bfloat16)
    word_at = lax.broadcasted_iota(jnp.int32, (LANES, LANES), 0)
    row_at = lax.broadcasted_iota(jnp.int32, (LANES, LANES), 1)
    which = lax.broadcasted_iota(jnp.int32, (4, LANES), 0)
    own_rows = which == lax.broadcasted_iota(jnp.int32, (4, LANES), 1) // 32
    adapter = lax.dot_general(
        own_up[...], own_down[...], (((0,), (0,)), ((), ())), preferred_element_type=jnp.float32
    )
    gains = gain[...].astype(jnp.float32).reshape(64, LANES)
    is_own = lax.broadcasted_iota(jnp.int32, gains.shape, 0) == shard
    gain_row = jnp.sum(jnp.where(is_own, gains, 0.0), axis=0, keepdims=True)
    pieces = []
    for q in range(2):
        pick = (word_at == 4 * (row_at % 32) + (2 * core + q)).astype(jnp.float32)
        found = jnp.dot(
            code_bytes, pick.astype(jnp.bfloat16), preferred_element_type=jnp.float32
        )
        for j in range(4):
            code = jnp.sum(
                jnp.where(own_rows, found[4 * j : 4 * j + 4], 0.0), axis=0, keepdims=True
            )
            absmax = (code + 0.5) / 256.0 * second
            block = 4 * q + j
            rows = slice(64 * block, 64 * block + 64)
            weight = levels[rows, :] * absmax + adapter_scale * adapter[rows]
            pieces.append((weight * gain_row).astype(jnp.bfloat16))
    whole[...] = jnp.concatenate(pieces, axis=0)


def decode(words, scale_words, outer, gain, down, up):
    return pl.pallas_call(
        decode_kernel,
        in_specs=[SMEM, ANY, VMEM, VMEM, ANY, ANY],
        out_specs=VMEM,
        out_shape=shape((HALF, LANES), jnp.bfloat16),
        scratch_shapes=[
            pltpu.VMEM((HALF, LANES), jnp.float32),
            pltpu.VMEM((LANES, LANES), jnp.int32),
            pltpu.VMEM((64, LANES), jnp.bfloat16),
            pltpu.VMEM((64, HALF), jnp.bfloat16),
            pltpu.SemaphoreType.DMA((3,)),
        ],
    )(outer, words, scale_words, gain, down.T, up)


def ring_offset(core, j):
    step = 1 - 2 * core
    return jnp.where(j == 0, 0, jnp.where(j == 1, -step, jnp.where(j == 2, step, 2)))


ROWS = 256
STEPS = 4


class Layout:
    def __init__(self, place):
        self.core, own = place[0], place[1]
        self.position = {ZH: own // 16, X: (own // 4) % 4, Y: own % 4}

    def features(self, arrival, part):
        middle, last = ORDER[part]
        at = (self.position[last] + ring_offset(self.core, arrival)) % 4 * STRIDE[last]
        width = 4 if middle == Y else 1
        for spot in range(0, 16, width):
            shard = spot // 4 * 16 + spot % 4 * STRIDE[middle] + at
            yield pl.multiple_of(shard * LANES, width * LANES), width * LANES

    def slots(self, part):
        middle, _ = ORDER[part]

        def slot(axis, place):
            ahead = (place - self.position[axis]) % 4
            step = (1 - 2 * self.core) % 4
            return jnp.where(
                ahead == 0, 0, jnp.where(ahead == 2, 3, jnp.where(ahead == step, 2, 1))
            )

        return [slot(middle, m) * 4 + slot(ZH, zh) for zh in range(4) for m in range(4)]


def product(left, weight, slots):
    right = jnp.concatenate([weight[slot] for slot in slots], axis=1)
    return lax.dot_general(
        left, right, (((1,), (1,)), ((), ())), preferred_element_type=jnp.float32
    )


def rows_of(width):
    return pl.BlockSpec((ROWS, width), lambda i, place: (i, 0))


def by_core(place):
    return place[0]


def rows_of_own(width, column=lambda place: 0):
    return pl.BlockSpec(
        (ROWS, width), lambda i, place: (jnp.minimum(i, STEPS // 2 - 1), column(place))
    )


def rows_of_other(width, column=lambda place: 0):
    return pl.BlockSpec(
        (ROWS, width), lambda i, place: (jnp.maximum(i - STEPS // 2, 0), column(place))
    )


def whole_weight():
    return pl.BlockSpec((16, PART, LANES), lambda i, place: (0, 0, 0))


def on_own_or_other(own, other, body):
    @pl.when(pl.program_id(0) < STEPS // 2)
    def _():
        body(*own)

    @pl.when(pl.program_id(0) >= STEPS // 2)
    def _():
        body(*other)


def taken(x, layout, arrival, part):
    return jnp.concatenate(
        [x[:, pl.ds(*run)] for run in layout.features(arrival, part)], axis=1
    )


def first_kernel(place, x0, x1, wb, wc, total, last):
    layout = Layout(place)
    depth = 16 * LANES

    def body(x):
        for part, weight in enumerate((wb, wc)):
            columns = slice(part * PART, (part + 1) * PART)
            total[:, columns] = product(
                taken(x, layout, 0, part), weight, layout.slots(part)
            )
            at = part * depth
            for start, width in layout.features(3, part):
                last[:, at : at + width] = x[:, pl.ds(start, width)]
                at += width

    on_own_or_other((x0,), (x1,), body)


def squares_kernel(x, squares):
    sums = jnp.zeros(squares.shape, jnp.float32)
    for k in range(0, x.shape[1], LANES):
        v = x[:, k : k + LANES].astype(jnp.float32)
        sums += v * v
    squares[...] = sums


def sum_squares(x):
    tokens, width = x.shape
    return pl.pallas_call(
        squares_kernel,
        grid=(8,),
        in_specs=[pl.BlockSpec((tokens // 8, width), lambda i: (i, 0))],
        out_specs=pl.BlockSpec((tokens // 8, LANES), lambda i: (i, 0)),
        out_shape=shape((tokens, LANES), jnp.float32),
        compiler_params=params(58),
    )(x)


def estimate(tokens, chunks):
    depth = 16 * LANES
    return pl.CostEstimate(
        flops=4 * tokens * chunks * depth * PART,
        transcendentals=0,
        bytes_accessed=4 * tokens * chunks * depth + 16 * tokens * HALF,
    )


def first(place, x, weights):
    tokens, width = x[0].shape
    depth = 2 * 16 * LANES
    return pl.pallas_call(
        first_kernel,
        grid_spec=pltpu.PrefetchScalarGridSpec(
            num_scalar_prefetch=1,
            grid=(STEPS,),
            in_specs=[rows_of_own(width), rows_of_other(width)] + [whole_weight()] * 2,
            out_specs=[rows_of(HALF), rows_of(depth)],
        ),
        out_shape=[
            shape((2 * tokens, HALF), jnp.float32),
            shape((2 * tokens, depth), jnp.bfloat16),
        ],
        compiler_params=params(34),
        cost_estimate=estimate(tokens, 4),
    )(place, *x, *weights)


def next_kernel(place, x0, x1, wb1, wc1, wb2, wc2, before, total):
    layout = Layout(place)

    def body(x):
        for part, weights in enumerate(((wb1, wb2), (wc1, wc2))):
            columns = slice(part * PART, (part + 1) * PART)
            value = before[:, columns]
            for arrival, weight in enumerate(weights, 1):
                value += product(taken(x, layout, arrival, part), weight, layout.slots(part))
            total[:, columns] = value

    on_own_or_other((x0,), (x1,), body)


def following(place, x, weights, before):
    tokens, width = x[0].shape
    flat = [w for pair in weights for w in pair]
    return pl.pallas_call(
        next_kernel,
        grid_spec=pltpu.PrefetchScalarGridSpec(
            num_scalar_prefetch=1,
            grid=(STEPS,),
            in_specs=[rows_of_own(width), rows_of_other(width)]
            + [whole_weight()] * 4
            + [rows_of(HALF)],
            out_specs=rows_of(HALF),
        ),
        out_shape=shape((2 * tokens, HALF), jnp.float32),
        compiler_params=params(40),
        cost_estimate=estimate(tokens, 4),
    )(place, *x, *flat, before)


def last_kernel(
    place, x, wb, wc, before, squares0, squares1, t0, t1, kv, other_kv, errors, sums
):
    layout = Layout(place)
    step = pl.program_id(0)

    @pl.when(step == 0)
    def _():
        sums[...] = jnp.zeros_like(sums)

    width = 2 * x.shape[1]
    depth = 16 * LANES

    def body(squares, target, out):
        mean = jnp.sum(squares[...], axis=1, keepdims=True) / width
        scale = lax.rsqrt(mean + epsilon)
        for part, weight in enumerate((wb, wc)):
            columns = slice(part * PART, (part + 1) * PART)
            value = product(
                x[:, part * depth : (part + 1) * depth], weight, layout.slots(part)
            )
            exact = (before[:, columns] + value) * scale
            out[:, columns] = exact.astype(jnp.bfloat16)
            error = exact - target[:, columns].astype(jnp.float32)
            error = error * error
            error = error[:, :LANES] + error[:, LANES:]
            sums[...] += jnp.sum(error.reshape(-1, 8, LANES), axis=0)

    on_own_or_other((squares0, t0, kv), (squares1, t1, other_kv), body)

    @pl.when(step == STEPS - 1)
    def _():
        errors[...] = jnp.broadcast_to(jnp.sum(sums[...], axis=0, keepdims=True), errors.shape)


def finish(place, x, weights, before, squares, targets):
    tokens, depth = x.shape[0] // 2, x.shape[1]
    return pl.pallas_call(
        last_kernel,
        grid_spec=pltpu.PrefetchScalarGridSpec(
            num_scalar_prefetch=1,
            grid=(STEPS,),
            in_specs=[rows_of(depth)]
            + [whole_weight()] * 2
            + [rows_of(HALF)]
            + [rows_of_own(LANES), rows_of_other(LANES)]
            + [rows_of_own(HALF, by_core), rows_of_other(HALF, by_core)],
            out_specs=[
                rows_of_own(HALF, by_core),
                rows_of_other(HALF),
                pl.BlockSpec((32, LANES), lambda i, place: (0, 0)),
            ],
            scratch_shapes=[pltpu.VMEM((8, LANES), jnp.float32)],
        ),
        out_shape=[
            shape((tokens, 2 * HALF), jnp.bfloat16),
            shape((tokens, HALF), jnp.bfloat16),
            shape((32, LANES), jnp.float32),
        ],
        compiler_params=params(26),
        cost_estimate=estimate(tokens, 2),
    )(place, x, *weights, before, *squares, *targets)


def swap_rows(everyone, groups):
    return lax.all_to_all(everyone, AXES, 0, 0, axis_index_groups=groups, tiled=True)


def spread_kernel(rows, out):
    out[...] = jnp.broadcast_to(jnp.sum(rows[...], axis=0, keepdims=True), out.shape)


def per_device(
    layer_input_rows,
    input_norm_gain,
    key_value_codes,
    block_scale_codes,
    outer_scale_codes,
    adapter_down_factor,
    adapter_up_factor,
    target,
):
    core = lax.axis_index("grp") % 2
    shard = lax.axis_index("fsdp")

    tokens = layer_input_rows.shape[0]
    other_rows = lax.ppermute(layer_input_rows, AXES, OTHER_CORE)
    place = jnp.stack([core, shard]).astype(jnp.int32)
    other_target = lax.ppermute(target, AXES, OTHER_CORE)

    own_weight = decode(
        key_value_codes,
        block_scale_codes,
        outer_scale_codes,
        input_norm_gain,
        adapter_down_factor,
        adapter_up_factor,
    )
    own_rows, own_weight = lax.optimization_barrier((layer_input_rows, own_weight))
    own_squares = sum_squares(own_rows)
    along_z = ring(own_weight, ZH)
    own_squares, other_target, *along_z = lax.optimization_barrier(
        (own_squares, other_target, *along_z)
    )
    squares = (own_squares, lax.ppermute(own_squares, AXES, OTHER_CORE))
    planes = []
    for part, (middle, last) in enumerate(ORDER):
        columns = slice(part * PART, (part + 1) * PART)
        line = jnp.stack([piece[columns] for piece in along_z])
        planes.append(jnp.concatenate(ring(line, middle)))

    behind = [lax.ppermute(p, AXES, FORWARD[last]) for p, (_, last) in zip(planes, ORDER)]
    ahead = [lax.ppermute(p, AXES, BACKWARD[last]) for p, (_, last) in zip(planes, ORDER)]
    x = (layer_input_rows, other_rows)
    total, last_x = first(place, x, planes)
    total, *behind = lax.optimization_barrier((total, *behind))
    opposite = [lax.ppermute(p, AXES, FORWARD[last]) for p, (_, last) in zip(behind, ORDER)]
    total = following(place, x, [behind, ahead], total)
    kv, other_kv, errors = finish(
        place, last_x, opposite, total, squares, (target, other_target)
    )
    received = lax.ppermute(other_kv, AXES, OTHER_CORE)
    kv = lax.dynamic_update_slice(kv, received, (0, (1 - core) * HALF))

    sums = swap_rows(errors, LOSS_GROUPS[0])
    sums = pl.pallas_call(
        spread_kernel, in_specs=[VMEM], out_specs=VMEM, out_shape=shape((8, LANES), jnp.float32)
    )(sums)
    sums = swap_rows(sums, LOSS_GROUPS[1])
    loss = jnp.sum(sums) / (tokens * lax.axis_size("fsdp") * 2 * HALF)
    return kv, loss


def solution(mesh):
    placed = (
        P(("grp", "fsdp"), None),
        P(),
        P("fsdp", None),
        P("fsdp", None),
        P("fsdp"),
        P(),
        P(),
        P(("grp", "fsdp"), None),
    )
    return jax.shard_map(
        per_device,
        mesh=mesh,
        in_specs=placed,
        out_specs=(P(("grp", "fsdp"), None), P()),
        check_vma=False,
    )
```

time: 304 us -> 121 us (0.40)
  waiting for transfers between devices: 223 us -> 20.9 us
  starting transfers between devices: 0.04 us -> 46.9 us
  Pallas kernels: 0 us -> 36.8 us
  matrix products: 24.7 us -> 0 us
  blocking collectives: 29.2 us -> 11.4 us
  between operations: 14.8 us -> 2.61 us
  other arithmetic: 9.34 us -> 0.76 us
    all_gather x1 -> x0, waiting for transfers between devices: 223 us -> none  [per_device(): lax.all_gather(owned, 'fsdp', axis=0, tiled=True)]
    ppermute x0 -> x19, starting transfers between devices: none -> 41.7 us  [the longest x4 15.9 us: per_device(): lax.ppermute(p, AXES, FORWARD[last])]
    pallas_call x0 -> x6, Pallas kernels: none -> 36.8 us  [the longest x1 10.9 us: following(): pl.pallas_call(next_kernel, grid_spec=pltpu.PrefetchScalarGridSpec(num_sc...]
    dot_general x2 -> x0, matrix products: 24.7 us -> none  [the longest x1 16.8 us: per_device(): jnp.dot(normed_input, lax.all_gather(owned, 'fsdp', axis=0, tiled=True),...]
    all_to_all x2 -> x1, blocking collectives: 29.2 us -> 11.4 us  [swap_rows(): lax.all_to_all(everyone, AXES, 0, 0, axis_index_groups=groups, tiled=True)]
    ppermute x0 -> x19, waiting for transfers between devices: none -> 14.4 us  [the longest x4 10 us: per_device(): lax.ppermute(p, AXES, FORWARD[last])]
    all_to_all x0 -> x1, waiting for transfers between devices: none -> 6.52 us  [swap_rows(): lax.all_to_all(everyone, AXES, 0, 0, axis_index_groups=groups, tiled=True)]
    reduce_sum x3 -> x1, other arithmetic: 6.37 us -> 0.61 us  [per_device(): loss = jnp.sum(sums) / (tokens * lax.axis_size('fsdp') * 2 * HALF)]
  transfers between devices with their start and end apart: 1 -> 20, of which waited for: 1 -> 8; matrix products, arithmetic and copies ran while one was open for 5% -> 1% of each run, Pallas kernels for 0% -> 26%
where the time goes in v2:
time: 121 us
  starting transfers between devices  46.9 us (39%)
  Pallas kernels  36.8 us (30%)
  waiting for transfers between devices  20.9 us (17%)
  blocking collectives  11.4 us (9%)
  between operations  2.61 us (2%)
    ppermute x4, starting transfers between devices, per_device(): lax.ppermute(p, AXES, FORWARD[last])  15.9 us
    all_to_all x1, blocking collectives, swap_rows(): lax.all_to_all(everyone, AXES, 0, 0, axis_index_groups=groups, tiled=True)  11.4 us
    pallas_call x1, Pallas kernels, following(): pl.pallas_call(next_kernel, grid_spec=pltpu.PrefetchScalarGridSpec(num_sc...  10.9 us
    ppermute x4, waiting for transfers between devices, per_device(): lax.ppermute(p, AXES, FORWARD[last])  10 us
    ppermute x3, starting transfers between devices, ring(): behind = lax.ppermute(block, AXES, FORWARD[axis])  9.73 us
    pallas_call x1, Pallas kernels, first(): pl.pallas_call(first_kernel, grid_spec=pltpu.PrefetchScalarGridSpec(num_s...  9.49 us
    pallas_call x1, Pallas kernels, sum_squares(): pl.pallas_call(squares_kernel, grid=(8,), in_specs=[pl.BlockSpec((tokens...  7.32 us
    all_to_all x1, waiting for transfers between devices, swap_rows(): lax.all_to_all(everyone, AXES, 0, 0, axis_index_groups=groups, tiled=True)  6.52 us
  transfers between devices with their start and end apart: 20, of which 8 were waited for; matrix products, arithmetic and copies ran while one was open for 1% of the time, Pallas kernels for 26%

profile of v2, /device:TPU:1, one launch (start us, length us, event | category | flops | bytes accessed | tf_op | source)
XLA Modules:
  0.0 120.5 jit_solution(7635021509253565108)
XLA Ops:
  0.6 3.3 %collective-permute-start = (bf16[512,8192]{1,0:T(8,128)(2,1)}, bf16[512,8192]{1,0:T(8,128)(2,1)}, u32[]{:S(2)}, u32[]{:S(2)}) collective-permute-start(bf16[512,8192]{1,0:T(8,128)(2,1)} %x0.3), channel_id=1, source_target_pairs={{0,64},{1,65},{2,66},{3,67},{4,68},{5,69},{6,70},{7,71},{8,72},{9,... | collective-permute-start | bytes 25165832 | tf_op jit(solution)/shard_map/ppermute | solution.py:443
  4.0 0.1 collective-permute-start.1
  4.1 2.8 %shard_map.95 = bf16[512,128]{1,0:T(8,128)(2,1)} custom-call(s32[8]{0:T(128)} %outer.1, s32[128,256]{1,0:T(8,128)} %words.1, s32[4,128]{1,0:T(4,128)} %scale_words.1, bf16[8192]{0:T(1024)(128)(2,1)} %gain.1, bf16[64,8192]{1,0:T(8,128)(2,1)} %bitcast.43, bf16[64,1024]{1,0:T(8,128)(2,1)} %up.1), custom_call_target="tpu_custom_call" | custom-call | tf_op jit(solution)/shard_map/pallas_call | solution.py:160
  6.9 4.4 %collective-permute-start.2 = (bf16[512,128]{1,0:T(8,128)(2,1)}, bf16[512,128]{1,0:T(8,128)(2,1)S(1)}, u32[]{:S(2)}, u32[]{:S(2)}) collective-permute-start(bf16[512,128]{1,0:T(8,128)(2,1)} %shard_map.95), channel_id=1, source_target_pairs={{0,16},{1,17},{2,18},{3,19},{4,20},{5,21},{6,22},{7,23},{8,24},{9,... | collective-permute-start | bytes 393224 | tf_op jit(solution)/shard_map/ppermute | solution.py:68
  11.2 0.0 collective-permute-start.3
  11.2 2.8 %collective-permute-start.4 = (bf16[512,128]{1,0:T(8,128)(2,1)}, bf16[512,128]{1,0:T(8,128)(2,1)S(1)}, u32[]{:S(2)}, u32[]{:S(2)}) collective-permute-start(bf16[512,128]{1,0:T(8,128)(2,1)} %shard_map.95), channel_id=1, source_target_pairs={{0,160},{1,161},{2,162},{3,163},{4,164},{5,165},{6,166},{7,167},{8... | collective-permute-start | bytes 393224 | tf_op jit(solution)/shard_map/ppermute | solution.py:71
  14.1 7.3 %shard_map.96.squares0 = f32[512,128]{1,0:T(8,128)} custom-call(bf16[512,8192]{1,0:T(8,128)(2,1)} %x0.3), custom_call_target="tpu_custom_call" | custom-call | tf_op jit(solution)/shard_map/pallas_call | solution.py:285
  21.4 0.0 collective-permute-done.2
  21.4 0.0 collective-permute-done.3
  21.4 2.2 %collective-permute-done.4 = bf16[512,128]{1,0:T(8,128)(2,1)S(1)} collective-permute-done((bf16[512,128]{1,0:T(8,128)(2,1)}, bf16[512,128]{1,0:T(8,128)(2,1)S(1)}, u32[]{:S(2)}, u32[]{:S(2)}) %collective-permute-start.4) | collective-permute-done | bytes 131104 | tf_op jit(solution)/shard_map/ppermute | solution.py:71
  23.6 0.0 collective-permute-done.1.t1
  23.7 2.6 %collective-permute-start.8 = (bf16[4,256,128]{2,1,0:T(8,128)(2,1)S(1)}, bf16[4,256,128]{2,1,0:T(8,128)(2,1)S(1)}, u32[]{:S(2)}, u32[]{:S(2)}) collective-permute-start(bf16[4,256,128]{2,1,0:T(8,128)(2,1)S(1)} %pad_maximum_fusion.1), channel_id=1, source_target_pairs={{0,4},{1,5},{2,6},{3,7},{4,8},{5,9},{6,10},{7,11},{8,12},{9,13},{1... | collective-permute-start | bytes 786440 | tf_op jit(solution)/shard_map/ppermute | solution.py:68
  26.3 0.0 collective-permute-start.9
  26.3 2.8 %collective-permute-start.5 = (bf16[4,256,128]{2,1,0:T(8,128)(2,1)S(1)}, bf16[4,256,128]{2,1,0:T(8,128)(2,1)S(1)}, u32[]{:S(2)}, u32[]{:S(2)}) collective-permute-start(bf16[4,256,128]{2,1,0:T(8,128)(2,1)S(1)} %pad_maximum_fusion), channel_id=1, source_target_pairs={{0,1},{1,2},{2,3},{3,0},{4,5},{5,6},{6,7},{7,4},{8,9},{9,10},{10,1... | collective-permute-start | bytes 786440 | tf_op jit(solution)/shard_map/ppermute | solution.py:68
  29.1 0.0 collective-permute-start.6
  29.2 1.8 %collective-permute-done.8 = bf16[4,256,128]{2,1,0:T(8,128)(2,1)S(1)} collective-permute-done((bf16[4,256,128]{2,1,0:T(8,128)(2,1)S(1)}, bf16[4,256,128]{2,1,0:T(8,128)(2,1)S(1)}, u32[]{:S(2)}, u32[]{:S(2)}) %collective-permute-start.8) | collective-permute-done | bytes 262176 | tf_op jit(solution)/shard_map/ppermute | solution.py:68
  31.1 3.4 %collective-permute-start.10 = (bf16[4,256,128]{2,1,0:T(8,128)(2,1)S(1)}, bf16[4,256,128]{2,1,0:T(8,128)(2,1)S(1)}, u32[]{:S(2)}, u32[]{:S(2)}) collective-permute-start(bf16[4,256,128]{2,1,0:T(8,128)(2,1)S(1)} %collective-permute-done.8), channel_id=1, source_target_pairs={{0,4},{1,5},{2,6},{3,7},{4,8},{5,9},{6,10},{7,11},{8,12},{9,13},{1... | collective-permute-start | bytes 786440 | tf_op jit(solution)/shard_map/ppermute | solution.py:73
  34.5 0.0 collective-permute-done.5
  34.5 2.8 %collective-permute-start.7 = (bf16[4,256,128]{2,1,0:T(8,128)(2,1)S(1)}, bf16[4,256,128]{2,1,0:T(8,128)(2,1)S(1)}, u32[]{:S(2)}, u32[]{:S(2)}) collective-permute-start(bf16[4,256,128]{2,1,0:T(8,128)(2,1)S(1)} %collective-permute-done.5), channel_id=1, source_target_pairs={{0,1},{1,2},{2,3},{3,0},{4,5},{5,6},{6,7},{7,4},{8,9},{9,10},{10,1... | collective-permute-start | bytes 786440 | tf_op jit(solution)/shard_map/ppermute | solution.py:73
  37.4 0.0 collective-permute-done.9
  37.4 0.1 collective-permute-done.6
  37.6 0.2 collective-permute-done.10
  37.8 2.8 %collective-permute-start.12 = (bf16[16,256,128]{2,1,0:T(8,128)(2,1)S(1)}, bf16[16,256,128]{2,1,0:T(8,128)(2,1)}, u32[]{:S(2)}, u32[]{:S(2)}) collective-permute-start(bf16[16,256,128]{2,1,0:T(8,128)(2,1)S(1)} %constant_dynamic-update-slice_fusion.7.wc), channel_id=1, source_target_pairs={{0,1},{1,2},{2,3},{3,0},{4,5},{5,6},{6,7},{7,4},{8,9},{9,10},{10,1... | collective-permute-start | bytes 3145736 | tf_op jit(solution)/shard_map/ppermute | solution.py:468
  40.6 0.0 collective-permute-done.7
  40.7 3.8 %collective-permute-start.11 = (bf16[16,256,128]{2,1,0:T(8,128)(2,1)S(1)}, bf16[16,256,128]{2,1,0:T(8,128)(2,1)}, u32[]{:S(2)}, u32[]{:S(2)}) collective-permute-start(bf16[16,256,128]{2,1,0:T(8,128)(2,1)S(1)} %constant_dynamic-update-slice_fusion.wb), channel_id=1, source_target_pairs={{0,4},{1,5},{2,6},{3,7},{4,8},{5,9},{6,10},{7,11},{8,12},{9,13},{1... | collective-permute-start | bytes 3145736 | tf_op jit(solution)/shard_map/ppermute | solution.py:468
  44.5 0.1 pad_add_fusion.place
  44.5 0.0 collective-permute-start.16
  44.6 0.3 collective-permute-start.15
  44.8 0.0 collective-permute-done.x1
  44.8 9.5 %shard_map.97 = (f32[1024,512]{1,0:T(8,128)S(1)}, bf16[1024,4096]{1,0:T(8,128)(2,1)S(1)}) custom-call(s32[2]{0:T(128)S(1)} %pad_add_fusion.place, bf16[512,8192]{1,0:T(8,128)(2,1)} %x0.3, bf16[512,8192]{1,0:T(8,128)(2,1)} %collective-permute-done.x1, bf16[16,256,128]{2,1,0:T(8,128)(2,1)S(1)} %constant_dynamic-update-slice_fusion.wb, ...), custom_call_target="tpu_custom_call" | custom-call | flops 4294967296 | bytes 20971520 | tf_op jit(solution)/shard_map/pallas_call | solution.py:307
  54.3 4.0 %collective-permute-done.12.wc1 = bf16[16,256,128]{2,1,0:T(8,128)(2,1)} collective-permute-done((bf16[16,256,128]{2,1,0:T(8,128)(2,1)S(1)}, bf16[16,256,128]{2,1,0:T(8,128)(2,1)}, u32[]{:S(2)}, u32[]{:S(2)}) %collective-permute-start.12) | collective-permute-done | bytes 1048608 | tf_op jit(solution)/shard_map/ppermute | solution.py:468
  58.3 4.9 %collective-permute-done.11.wb1 = bf16[16,256,128]{2,1,0:T(8,128)(2,1)} collective-permute-done((bf16[16,256,128]{2,1,0:T(8,128)(2,1)S(1)}, bf16[16,256,128]{2,1,0:T(8,128)(2,1)}, u32[]{:S(2)}, u32[]{:S(2)}) %collective-permute-start.11) | collective-permute-done | bytes 1048608 | tf_op jit(solution)/shard_map/ppermute | solution.py:468
  63.2 3.4 %collective-permute-start.13 = (bf16[16,256,128]{2,1,0:T(8,128)(2,1)}, bf16[16,256,128]{2,1,0:T(8,128)(2,1)S(1)}, u32[]{:S(2)}, u32[]{:S(2)}) collective-permute-start(bf16[16,256,128]{2,1,0:T(8,128)(2,1)} %collective-permute-done.11.wb1), channel_id=1, source_target_pairs={{0,4},{1,5},{2,6},{3,7},{4,8},{5,9},{6,10},{7,11},{8,12},{9,13},{1... | collective-permute-start | bytes 3145736 | tf_op jit(solution)/shard_map/ppermute | solution.py:473
  66.6 5.9 %collective-permute-start.14 = (bf16[16,256,128]{2,1,0:T(8,128)(2,1)}, bf16[16,256,128]{2,1,0:T(8,128)(2,1)S(1)}, u32[]{:S(2)}, u32[]{:S(2)}) collective-permute-start(bf16[16,256,128]{2,1,0:T(8,128)(2,1)} %collective-permute-done.12.wc1), channel_id=1, source_target_pairs={{0,1},{1,2},{2,3},{3,0},{4,5},{5,6},{6,7},{7,4},{8,9},{9,10},{10,1... | collective-permute-start | bytes 3145736 | tf_op jit(solution)/shard_map/ppermute | solution.py:473
  72.5 0.0 collective-permute-start.17
  72.5 0.0 collective-permute-done.16.wc2
  72.5 10.9 %shard_map.98.before = f32[1024,512]{1,0:T(8,128)S(1)} custom-call(s32[2]{0:T(128)S(1)} %pad_add_fusion.place, bf16[512,8192]{1,0:T(8,128)(2,1)} %x0.3, bf16[512,8192]{1,0:T(8,128)(2,1)} %collective-permute-done.x1, bf16[16,256,128]{2,1,0:T(8,128)(2,1)} %collective-permute-done.11.wb1, bf16[16,256,128]{2,1,0:T(8,128)(2,1)} %collective-permute-done.12.wc1, ...), custom_call_target="tpu_custom_call" | custom-call | flops 4294967296 | bytes 20971520 | tf_op jit(solution)/shard_map/pallas_call | solution.py:341
  83.4 0.0 collective-permute-done.13.wb
  83.4 1.1 collective-permute-done.14.wc
  84.6 5.0 %shard_map.99 = (bf16[512,1024]{1,0:T(8,128)(2,1)}, bf16[512,512]{1,0:T(8,128)(2,1)S(1)}, f32[32,128]{1,0:T(8,128)S(1)}) custom-call(s32[2]{0:T(128)S(1)} %pad_add_fusion.place, bf16[1024,4096]{1,0:T(8,128)(2,1)S(1)} %get-tuple-element.24.x, bf16[16,256,128]{2,1,0:T(8,128)(2,1)S(1)} %collective-permute-done.13.wb, ...), custom_call_target="tpu_custom_call" | custom-call | flops 2147483648 | bytes 12582912 | tf_op jit(solution)/shard_map/pallas_call | solution.py:394
  89.5 3.4 %collective-permute-start.18 = (bf16[512,512]{1,0:T(8,128)(2,1)S(1)}, bf16[512,512]{1,0:T(8,128)(2,1)S(1)}, u32[]{:S(2)}, u32[]{:S(2)}) collective-permute-start(bf16[512,512]{1,0:T(8,128)(2,1)S(1)} %get-tuple-element.32), channel_id=1, source_target_pairs={{0,64},{1,65},{2,66},{3,67},{4,68},{5,69},{6,70},{7,71},{8,72},{9,... | collective-permute-start | bytes 1572872 | tf_op jit(solution)/shard_map/ppermute | solution.py:478
  92.9 11.4 %all_to_all.20 = f32[32,1,128]{2,1,0:T(1,128)} all-to-all(f32[32,1,128]{2,1,0:T(1,128)S(1)} %bitcast.42), channel_id=1, replica_groups={{0,1,2,3,4,5,6,7,8,9,10,11,12,13,14,15,64,65,66,67,68,69,70,71,72,73,74..., dimensions={0} | all-to-all | bytes 32768 | tf_op jit(solution)/shard_map/all_to_all | solution.py:422
  104.3 1.3 %shard_map.100 = f32[8,128]{1,0:T(8,128)} custom-call(f32[32,128]{1,0:T(8,128)} %bitcast.44), custom_call_target="tpu_custom_call" | custom-call | tf_op jit(solution)/shard_map/pallas_call | solution.py:482
  105.6 5.2 %all-to-all-start.1 = ((f32[8,1,128]{2,1,0:T(1,128)}), f32[8,1,128]{2,1,0:T(1,128)S(1)}, u32[]{:S(2)}, u32[]{:S(2)}) async-start(f32[8,1,128]{2,1,0:T(1,128)} %bitcast.45), calls=%async_computation.1 | async-start | bytes 8192 | tf_op jit(solution)/shard_map/all_to_all | solution.py:422
  110.8 6.5 %all-to-all-done.1 = f32[8,1,128]{2,1,0:T(1,128)S(1)} async-done(((f32[8,1,128]{2,1,0:T(1,128)}), f32[8,1,128]{2,1,0:T(1,128)S(1)}, u32[]{:S(2)}, u32[]{:S(2)}) %all-to-all-start.1) | async-done | bytes 4128 | tf_op jit(solution)/shard_map/all_to_all | solution.py:422
  117.3 0.6 reduce_sum.9
  118.6 0.0 collective-permute-done.18
  118.6 0.8 constant_dynamic-update-slice_fusion.14
  (22 shorter events, 0.4 us)
Async XLA Ops:
  0.6 44.2 %collective-permute-start = (bf16[512,8192]{1,0:T(8,128)(2,1)}, bf16[512,8192]{1,0:T(8,128)(2,1)}, u32[]{:S(2)}, u32[]{:S(2)}) collective-permute-start(bf16[512,8192]{1,0:T(8,128)(2,1)} %x0.3), channel_id=1, source_target_pairs={{0,64},{1,65},{2,66},{3,67},{4,68},{5,69},{6,70},{7,71},{8,72},{9,... | collective-permute-start | bytes 25165832 | tf_op jit(solution)/shard_map/ppermute | solution.py:443
  4.0 19.7 %collective-permute-start.1 = (bf16[512,1024]{1,0:T(8,128)(2,1)}, bf16[512,1024]{1,0:T(8,128)(2,1)S(1)}, u32[]{:S(2)}, u32[]{:S(2)}) collective-permute-start(bf16[512,1024]{1,0:T(8,128)(2,1)} %t0.1), channel_id=1, source_target_pairs={{0,64},{1,65},{2,66},{3,67},{4,68},{5,69},{6,70},{7,71},{8,72},{9,... | collective-permute-start | bytes 3145736 | tf_op jit(solution)/shard_map/ppermute | solution.py:445
  6.9 16.8 %copy-start.2 = (bf16[512,128]{1,0:T(8,128)(2,1)S(1)}, bf16[512,128]{1,0:T(8,128)(2,1)}, u32[]{:S(2)}) copy-start(bf16[512,128]{1,0:T(8,128)(2,1)} %shard_map.95) | copy-start | bytes 393220
  6.9 14.5 %collective-permute-start.2 = (bf16[512,128]{1,0:T(8,128)(2,1)}, bf16[512,128]{1,0:T(8,128)(2,1)S(1)}, u32[]{:S(2)}, u32[]{:S(2)}) collective-permute-start(bf16[512,128]{1,0:T(8,128)(2,1)} %shard_map.95), channel_id=1, source_target_pairs={{0,16},{1,17},{2,18},{3,19},{4,20},{5,21},{6,22},{7,23},{8,24},{9,... | collective-permute-start | bytes 393224 | tf_op jit(solution)/shard_map/ppermute | solution.py:68
  11.2 10.1 %collective-permute-start.3 = (bf16[512,128]{1,0:T(8,128)(2,1)}, bf16[512,128]{1,0:T(8,128)(2,1)S(1)}, u32[]{:S(2)}, u32[]{:S(2)}) collective-permute-start(bf16[512,128]{1,0:T(8,128)(2,1)} %shard_map.95), channel_id=1, source_target_pairs={{0,48},{1,49},{2,50},{3,51},{4,52},{5,53},{6,54},{7,55},{8,56},{9,... | collective-permute-start | bytes 393224 | tf_op jit(solution)/shard_map/ppermute | solution.py:69
  11.2 12.4 %collective-permute-start.4 = (bf16[512,128]{1,0:T(8,128)(2,1)}, bf16[512,128]{1,0:T(8,128)(2,1)S(1)}, u32[]{:S(2)}, u32[]{:S(2)}) collective-permute-start(bf16[512,128]{1,0:T(8,128)(2,1)} %shard_map.95), channel_id=1, source_target_pairs={{0,160},{1,161},{2,162},{3,163},{4,164},{5,165},{6,166},{7,167},{8... | collective-permute-start | bytes 393224 | tf_op jit(solution)/shard_map/ppermute | solution.py:71
  23.7 7.3 %collective-permute-start.8 = (bf16[4,256,128]{2,1,0:T(8,128)(2,1)S(1)}, bf16[4,256,128]{2,1,0:T(8,128)(2,1)S(1)}, u32[]{:S(2)}, u32[]{:S(2)}) collective-permute-start(bf16[4,256,128]{2,1,0:T(8,128)(2,1)S(1)} %pad_maximum_fusion.1), channel_id=1, source_target_pairs={{0,4},{1,5},{2,6},{3,7},{4,8},{5,9},{6,10},{7,11},{8,12},{9,13},{1... | collective-permute-start | bytes 786440 | tf_op jit(solution)/shard_map/ppermute | solution.py:68
  26.3 11.1 %collective-permute-start.9 = (bf16[4,256,128]{2,1,0:T(8,128)(2,1)S(1)}, bf16[4,256,128]{2,1,0:T(8,128)(2,1)S(1)}, u32[]{:S(2)}, u32[]{:S(2)}) collective-permute-start(bf16[4,256,128]{2,1,0:T(8,128)(2,1)S(1)} %pad_maximum_fusion.1), channel_id=1, source_target_pairs={{0,12},{1,13},{2,14},{3,15},{4,0},{5,1},{6,2},{7,3},{8,4},{9,5},{1... | collective-permute-start | bytes 786440 | tf_op jit(solution)/shard_map/ppermute | solution.py:69
  26.3 8.2 %collective-permute-start.5 = (bf16[4,256,128]{2,1,0:T(8,128)(2,1)S(1)}, bf16[4,256,128]{2,1,0:T(8,128)(2,1)S(1)}, u32[]{:S(2)}, u32[]{:S(2)}) collective-permute-start(bf16[4,256,128]{2,1,0:T(8,128)(2,1)S(1)} %pad_maximum_fusion), channel_id=1, source_target_pairs={{0,1},{1,2},{2,3},{3,0},{4,5},{5,6},{6,7},{7,4},{8,9},{9,10},{10,1... | collective-permute-start | bytes 786440 | tf_op jit(solution)/shard_map/ppermute | solution.py:68
  29.1 8.4 %collective-permute-start.6 = (bf16[4,256,128]{2,1,0:T(8,128)(2,1)S(1)}, bf16[4,256,128]{2,1,0:T(8,128)(2,1)S(1)}, u32[]{:S(2)}, u32[]{:S(2)}) collective-permute-start(bf16[4,256,128]{2,1,0:T(8,128)(2,1)S(1)} %pad_maximum_fusion), channel_id=1, source_target_pairs={{0,3},{1,0},{2,1},{3,2},{4,7},{5,4},{6,5},{7,6},{8,11},{9,8},{10,9... | collective-permute-start | bytes 786440 | tf_op jit(solution)/shard_map/ppermute | solution.py:69
  31.1 6.7 %collective-permute-start.10 = (bf16[4,256,128]{2,1,0:T(8,128)(2,1)S(1)}, bf16[4,256,128]{2,1,0:T(8,128)(2,1)S(1)}, u32[]{:S(2)}, u32[]{:S(2)}) collective-permute-start(bf16[4,256,128]{2,1,0:T(8,128)(2,1)S(1)} %collective-permute-done.8), channel_id=1, source_target_pairs={{0,4},{1,5},{2,6},{3,7},{4,8},{5,9},{6,10},{7,11},{8,12},{9,13},{1... | collective-permute-start | bytes 786440 | tf_op jit(solution)/shard_map/ppermute | solution.py:73
  34.5 6.1 %collective-permute-start.7 = (bf16[4,256,128]{2,1,0:T(8,128)(2,1)S(1)}, bf16[4,256,128]{2,1,0:T(8,128)(2,1)S(1)}, u32[]{:S(2)}, u32[]{:S(2)}) collective-permute-start(bf16[4,256,128]{2,1,0:T(8,128)(2,1)S(1)} %collective-permute-done.5), channel_id=1, source_target_pairs={{0,1},{1,2},{2,3},{3,0},{4,5},{5,6},{6,7},{7,4},{8,9},{9,10},{10,1... | collective-permute-start | bytes 786440 | tf_op jit(solution)/shard_map/ppermute | solution.py:73
  37.8 20.5 %collective-permute-start.12 = (bf16[16,256,128]{2,1,0:T(8,128)(2,1)S(1)}, bf16[16,256,128]{2,1,0:T(8,128)(2,1)}, u32[]{:S(2)}, u32[]{:S(2)}) collective-permute-start(bf16[16,256,128]{2,1,0:T(8,128)(2,1)S(1)} %constant_dynamic-update-slice_fusion.7.wc), channel_id=1, source_target_pairs={{0,1},{1,2},{2,3},{3,0},{4,5},{5,6},{6,7},{7,4},{8,9},{9,10},{10,1... | collective-permute-start | bytes 3145736 | tf_op jit(solution)/shard_map/ppermute | solution.py:468
  40.7 22.5 %collective-permute-start.11 = (bf16[16,256,128]{2,1,0:T(8,128)(2,1)S(1)}, bf16[16,256,128]{2,1,0:T(8,128)(2,1)}, u32[]{:S(2)}, u32[]{:S(2)}) collective-permute-start(bf16[16,256,128]{2,1,0:T(8,128)(2,1)S(1)} %constant_dynamic-update-slice_fusion.wb), channel_id=1, source_target_pairs={{0,4},{1,5},{2,6},{3,7},{4,8},{5,9},{6,10},{7,11},{8,12},{9,13},{1... | collective-permute-start | bytes 3145736 | tf_op jit(solution)/shard_map/ppermute | solution.py:468
  44.5 28.0 %copy-start = (f32[512,128]{1,0:T(8,128)S(1)}, f32[512,128]{1,0:T(8,128)}, u32[]{:S(2)}) copy-start(f32[512,128]{1,0:T(8,128)} %shard_map.96.squares0) | copy-start | bytes 786436
  44.5 28.0 %collective-permute-start.16 = (bf16[16,256,128]{2,1,0:T(8,128)(2,1)S(1)}, bf16[16,256,128]{2,1,0:T(8,128)(2,1)S(1)}, u32[]{:S(2)}, u32[]{:S(2)}) collective-permute-start(bf16[16,256,128]{2,1,0:T(8,128)(2,1)S(1)} %constant_dynamic-update-slice_fusion.7.wc), channel_id=1, source_target_pairs={{0,3},{1,0},{2,1},{3,2},{4,7},{5,4},{6,5},{7,6},{8,11},{9,8},{10,9... | collective-permute-start | bytes 3145736 | tf_op jit(solution)/shard_map/ppermute | solution.py:469
  44.6 28.0 %collective-permute-start.15 = (bf16[16,256,128]{2,1,0:T(8,128)(2,1)S(1)}, bf16[16,256,128]{2,1,0:T(8,128)(2,1)S(1)}, u32[]{:S(2)}, u32[]{:S(2)}) collective-permute-start(bf16[16,256,128]{2,1,0:T(8,128)(2,1)S(1)} %constant_dynamic-update-slice_fusion.wb), channel_id=1, source_target_pairs={{0,12},{1,13},{2,14},{3,15},{4,0},{5,1},{6,2},{7,3},{8,4},{9,5},{1... | collective-permute-start | bytes 3145736 | tf_op jit(solution)/shard_map/ppermute | solution.py:469
  63.2 21.4 %copy-start.1 = (bf16[512,1024]{1,0:T(8,128)(2,1)S(1)}, bf16[512,1024]{1,0:T(8,128)(2,1)}, u32[]{:S(2)}) copy-start(bf16[512,1024]{1,0:T(8,128)(2,1)} %t0.1) | copy-start | bytes 3145732
  63.2 20.2 %collective-permute-start.13 = (bf16[16,256,128]{2,1,0:T(8,128)(2,1)}, bf16[16,256,128]{2,1,0:T(8,128)(2,1)S(1)}, u32[]{:S(2)}, u32[]{:S(2)}) collective-permute-start(bf16[16,256,128]{2,1,0:T(8,128)(2,1)} %collective-permute-done.11.wb1), channel_id=1, source_target_pairs={{0,4},{1,5},{2,6},{3,7},{4,8},{5,9},{6,10},{7,11},{8,12},{9,13},{1... | collective-permute-start | bytes 3145736 | tf_op jit(solution)/shard_map/ppermute | solution.py:473
  66.6 18.0 %collective-permute-start.14 = (bf16[16,256,128]{2,1,0:T(8,128)(2,1)}, bf16[16,256,128]{2,1,0:T(8,128)(2,1)S(1)}, u32[]{:S(2)}, u32[]{:S(2)}) collective-permute-start(bf16[16,256,128]{2,1,0:T(8,128)(2,1)} %collective-permute-done.12.wc1), channel_id=1, source_target_pairs={{0,1},{1,2},{2,3},{3,0},{4,5},{5,6},{6,7},{7,4},{8,9},{9,10},{10,1... | collective-permute-start | bytes 3145736 | tf_op jit(solution)/shard_map/ppermute | solution.py:473
  72.5 10.9 %collective-permute-start.17 = (f32[512,128]{1,0:T(8,128)S(1)}, f32[512,128]{1,0:T(8,128)S(1)}, u32[]{:S(2)}, u32[]{:S(2)}) collective-permute-start(f32[512,128]{1,0:T(8,128)S(1)} %copy-done), channel_id=1, source_target_pairs={{0,64},{1,65},{2,66},{3,67},{4,68},{5,69},{6,70},{7,71},{8,72},{9,... | collective-permute-start | bytes 786440 | tf_op jit(solution)/shard_map/ppermute | solution.py:461
  89.5 29.0 %collective-permute-start.18 = (bf16[512,512]{1,0:T(8,128)(2,1)S(1)}, bf16[512,512]{1,0:T(8,128)(2,1)S(1)}, u32[]{:S(2)}, u32[]{:S(2)}) collective-permute-start(bf16[512,512]{1,0:T(8,128)(2,1)S(1)} %get-tuple-element.32), channel_id=1, source_target_pairs={{0,64},{1,65},{2,66},{3,67},{4,68},{5,69},{6,70},{7,71},{8,72},{9,... | collective-permute-start | bytes 1572872 | tf_op jit(solution)/shard_map/ppermute | solution.py:478
  105.6 11.7 %all-to-all-start.1 = ((f32[8,1,128]{2,1,0:T(1,128)}), f32[8,1,128]{2,1,0:T(1,128)S(1)}, u32[]{:S(2)}, u32[]{:S(2)}) async-start(f32[8,1,128]{2,1,0:T(1,128)} %bitcast.45), calls=%async_computation.1 | async-start | bytes 8192 | tf_op jit(solution)/shard_map/all_to_all | solution.py:422

commit v3 on v2

--- a/solution.py
+++ b/solution.py
@@ -483,6 +483,7 @@
         spread_kernel, in_specs=[VMEM], out_specs=VMEM, out_shape=shape((8, LANES), jnp.float32)
     )(sums)
     sums = swap_rows(sums, LOSS_GROUPS[1])
+    sums, kv = lax.optimization_barrier((sums, kv))
     loss = jnp.sum(sums) / (tokens * lax.axis_size("fsdp") * 2 * HALF)
     return kv, loss
 

time: 121 us -> 121 us (level)
  blocking collectives: 11.4 us -> 0 us
  waiting for transfers between devices: 20.9 us -> 26.8 us
  starting transfers between devices: 46.9 us -> 51.7 us
    all_to_all x1 -> x0, blocking collectives: 11.4 us -> none  [swap_rows(): lax.all_to_all(everyone, AXES, 0, 0, axis_index_groups=groups, tiled=True)]
    all_to_all x1 -> x2, waiting for transfers between devices: 6.52 us -> 12.4 us  [swap_rows(): lax.all_to_all(everyone, AXES, 0, 0, axis_index_groups=groups, tiled=True)]
    all_to_all x1 -> x2, starting transfers between devices: 5.18 us -> 9.97 us  [swap_rows(): lax.all_to_all(everyone, AXES, 0, 0, axis_index_groups=groups, tiled=True)]
  transfers between devices with their start and end apart: 20 -> 21, of which waited for: 8 -> 9; matrix products, arithmetic and copies ran while one was open for 1% -> 1% of each run, Pallas kernels for 26% -> 26%
where the time goes in v3:
time: 121 us; the launch traced here: 120 us
  starting transfers between devices  51.7 us (43%)
  Pallas kernels  36.8 us (30%)
  waiting for transfers between devices  26.8 us (22%)
  between operations  2.62 us (2%)
  local copies, waits for them, and re-layouts  1.77 us (1%)
    ppermute x4, starting transfers between devices, per_device(): lax.ppermute(p, AXES, FORWARD[last])  15.9 us
    all_to_all x2, waiting for transfers between devices, swap_rows(): lax.all_to_all(everyone, AXES, 0, 0, axis_index_groups=groups, tiled=True)  12.4 us
    pallas_call x1, Pallas kernels, following(): pl.pallas_call(next_kernel, grid_spec=pltpu.PrefetchScalarGridSpec(num_sc...  10.9 us
    ppermute x4, waiting for transfers between devices, per_device(): lax.ppermute(p, AXES, FORWARD[last])  10 us
    all_to_all x2, starting transfers between devices, swap_rows(): lax.all_to_all(everyone, AXES, 0, 0, axis_index_groups=groups, tiled=True)  9.97 us
    ppermute x3, starting transfers between devices, ring(): behind = lax.ppermute(block, AXES, FORWARD[axis])  9.73 us
    pallas_call x1, Pallas kernels, first(): pl.pallas_call(first_kernel, grid_spec=pltpu.PrefetchScalarGridSpec(num_s...  9.48 us
    pallas_call x1, Pallas kernels, sum_squares(): pl.pallas_call(squares_kernel, grid=(8,), in_specs=[pl.BlockSpec((tokens...  7.32 us
  transfers between devices with their start and end apart: 21, of which 9 were waited for; matrix products, arithmetic and copies ran while one was open for 1% of the time, Pallas kernels for 26%

profile of v3, /device:TPU:1, one launch (start us, length us, event | category | flops | bytes accessed | tf_op | source)
XLA Modules:
  0.0 120.4 jit_solution(6051956156635686561)
XLA Ops:
  0.6 3.3 %collective-permute-start = (bf16[512,8192]{1,0:T(8,128)(2,1)}, bf16[512,8192]{1,0:T(8,128)(2,1)}, u32[]{:S(2)}, u32[]{:S(2)}) collective-permute-start(bf16[512,8192]{1,0:T(8,128)(2,1)} %x0.3), channel_id=1, source_target_pairs={{0,64},{1,65},{2,66},{3,67},{4,68},{5,69},{6,70},{7,71},{8,72},{9,... | collective-permute-start | bytes 25165832 | tf_op jit(solution)/shard_map/ppermute | solution.py:443
  4.0 0.1 collective-permute-start.1
  4.1 2.8 %shard_map.95 = bf16[512,128]{1,0:T(8,128)(2,1)} custom-call(s32[8]{0:T(128)} %outer.1, s32[128,256]{1,0:T(8,128)} %words.1, s32[4,128]{1,0:T(4,128)} %scale_words.1, bf16[8192]{0:T(1024)(128)(2,1)} %gain.1, bf16[64,8192]{1,0:T(8,128)(2,1)} %bitcast.43, bf16[64,1024]{1,0:T(8,128)(2,1)} %up.1), custom_call_target="tpu_custom_call" | custom-call | tf_op jit(solution)/shard_map/pallas_call | solution.py:160
  6.9 4.4 %collective-permute-start.2 = (bf16[512,128]{1,0:T(8,128)(2,1)}, bf16[512,128]{1,0:T(8,128)(2,1)S(1)}, u32[]{:S(2)}, u32[]{:S(2)}) collective-permute-start(bf16[512,128]{1,0:T(8,128)(2,1)} %shard_map.95), channel_id=1, source_target_pairs={{0,16},{1,17},{2,18},{3,19},{4,20},{5,21},{6,22},{7,23},{8,24},{9,... | collective-permute-start | bytes 393224 | tf_op jit(solution)/shard_map/ppermute | solution.py:68
  11.2 0.0 collective-permute-start.3
  11.3 2.8 %collective-permute-start.4 = (bf16[512,128]{1,0:T(8,128)(2,1)}, bf16[512,128]{1,0:T(8,128)(2,1)S(1)}, u32[]{:S(2)}, u32[]{:S(2)}) collective-permute-start(bf16[512,128]{1,0:T(8,128)(2,1)} %shard_map.95), channel_id=1, source_target_pairs={{0,160},{1,161},{2,162},{3,163},{4,164},{5,165},{6,166},{7,167},{8... | collective-permute-start | bytes 393224 | tf_op jit(solution)/shard_map/ppermute | solution.py:71
  14.1 7.3 %shard_map.96.squares0 = f32[512,128]{1,0:T(8,128)} custom-call(bf16[512,8192]{1,0:T(8,128)(2,1)} %x0.3), custom_call_target="tpu_custom_call" | custom-call | tf_op jit(solution)/shard_map/pallas_call | solution.py:285
  21.4 0.0 collective-permute-done.2
  21.4 0.0 collective-permute-done.3
  21.4 2.2 %collective-permute-done.4 = bf16[512,128]{1,0:T(8,128)(2,1)S(1)} collective-permute-done((bf16[512,128]{1,0:T(8,128)(2,1)}, bf16[512,128]{1,0:T(8,128)(2,1)S(1)}, u32[]{:S(2)}, u32[]{:S(2)}) %collective-permute-start.4) | collective-permute-done | bytes 131104 | tf_op jit(solution)/shard_map/ppermute | solution.py:71
  23.6 0.0 collective-permute-done.1.t1
  23.7 2.6 %collective-permute-start.8 = (bf16[4,256,128]{2,1,0:T(8,128)(2,1)S(1)}, bf16[4,256,128]{2,1,0:T(8,128)(2,1)S(1)}, u32[]{:S(2)}, u32[]{:S(2)}) collective-permute-start(bf16[4,256,128]{2,1,0:T(8,128)(2,1)S(1)} %pad_maximum_fusion.1), channel_id=1, source_target_pairs={{0,4},{1,5},{2,6},{3,7},{4,8},{5,9},{6,10},{7,11},{8,12},{9,13},{1... | collective-permute-start | bytes 786440 | tf_op jit(solution)/shard_map/ppermute | solution.py:68
  26.3 2.8 %collective-permute-start.5 = (bf16[4,256,128]{2,1,0:T(8,128)(2,1)S(1)}, bf16[4,256,128]{2,1,0:T(8,128)(2,1)S(1)}, u32[]{:S(2)}, u32[]{:S(2)}) collective-permute-start(bf16[4,256,128]{2,1,0:T(8,128)(2,1)S(1)} %pad_maximum_fusion), channel_id=1, source_target_pairs={{0,1},{1,2},{2,3},{3,0},{4,5},{5,6},{6,7},{7,4},{8,9},{9,10},{10,1... | collective-permute-start | bytes 786440 | tf_op jit(solution)/shard_map/ppermute | solution.py:68
  29.2 0.0 collective-permute-start.6
  29.3 1.8 %collective-permute-done.8 = bf16[4,256,128]{2,1,0:T(8,128)(2,1)S(1)} collective-permute-done((bf16[4,256,128]{2,1,0:T(8,128)(2,1)S(1)}, bf16[4,256,128]{2,1,0:T(8,128)(2,1)S(1)}, u32[]{:S(2)}, u32[]{:S(2)}) %collective-permute-start.8) | collective-permute-done | bytes 262176 | tf_op jit(solution)/shard_map/ppermute | solution.py:68
  31.1 3.4 %collective-permute-start.10 = (bf16[4,256,128]{2,1,0:T(8,128)(2,1)S(1)}, bf16[4,256,128]{2,1,0:T(8,128)(2,1)S(1)}, u32[]{:S(2)}, u32[]{:S(2)}) collective-permute-start(bf16[4,256,128]{2,1,0:T(8,128)(2,1)S(1)} %collective-permute-done.8), channel_id=1, source_target_pairs={{0,4},{1,5},{2,6},{3,7},{4,8},{5,9},{6,10},{7,11},{8,12},{9,13},{1... | collective-permute-start | bytes 786440 | tf_op jit(solution)/shard_map/ppermute | solution.py:73
  34.5 2.8 %collective-permute-start.7 = (bf16[4,256,128]{2,1,0:T(8,128)(2,1)S(1)}, bf16[4,256,128]{2,1,0:T(8,128)(2,1)S(1)}, u32[]{:S(2)}, u32[]{:S(2)}) collective-permute-start(bf16[4,256,128]{2,1,0:T(8,128)(2,1)S(1)} %collective-permute-done.5), channel_id=1, source_target_pairs={{0,1},{1,2},{2,3},{3,0},{4,5},{5,6},{6,7},{7,4},{8,9},{9,10},{10,1... | collective-permute-start | bytes 786440 | tf_op jit(solution)/shard_map/ppermute | solution.py:73
  37.4 0.0 collective-permute-done.9
  37.4 0.1 collective-permute-done.6
  37.6 0.2 collective-permute-done.10
  37.8 2.8 %collective-permute-start.12 = (bf16[16,256,128]{2,1,0:T(8,128)(2,1)S(1)}, bf16[16,256,128]{2,1,0:T(8,128)(2,1)}, u32[]{:S(2)}, u32[]{:S(2)}) collective-permute-start(bf16[16,256,128]{2,1,0:T(8,128)(2,1)S(1)} %constant_dynamic-update-slice_fusion.7.wc), channel_id=1, source_target_pairs={{0,1},{1,2},{2,3},{3,0},{4,5},{5,6},{6,7},{7,4},{8,9},{9,10},{10,1... | collective-permute-start | bytes 3145736 | tf_op jit(solution)/shard_map/ppermute | solution.py:468
  40.6 0.0 collective-permute-done.7
  40.7 3.8 %collective-permute-start.11 = (bf16[16,256,128]{2,1,0:T(8,128)(2,1)S(1)}, bf16[16,256,128]{2,1,0:T(8,128)(2,1)}, u32[]{:S(2)}, u32[]{:S(2)}) collective-permute-start(bf16[16,256,128]{2,1,0:T(8,128)(2,1)S(1)} %constant_dynamic-update-slice_fusion.wb), channel_id=1, source_target_pairs={{0,4},{1,5},{2,6},{3,7},{4,8},{5,9},{6,10},{7,11},{8,12},{9,13},{1... | collective-permute-start | bytes 3145736 | tf_op jit(solution)/shard_map/ppermute | solution.py:468
  44.5 0.1 pad_add_fusion.place
  44.5 0.0 collective-permute-start.16
  44.6 0.3 collective-permute-start.15
  44.8 0.0 collective-permute-done.x1
  44.8 9.5 %shard_map.97 = (f32[1024,512]{1,0:T(8,128)S(1)}, bf16[1024,4096]{1,0:T(8,128)(2,1)S(1)}) custom-call(s32[2]{0:T(128)S(1)} %pad_add_fusion.place, bf16[512,8192]{1,0:T(8,128)(2,1)} %x0.3, bf16[512,8192]{1,0:T(8,128)(2,1)} %collective-permute-done.x1, bf16[16,256,128]{2,1,0:T(8,128)(2,1)S(1)} %constant_dynamic-update-slice_fusion.wb, ...), custom_call_target="tpu_custom_call" | custom-call | flops 4294967296 | bytes 20971520 | tf_op jit(solution)/shard_map/pallas_call | solution.py:307
  54.3 4.0 %collective-permute-done.12.wc1 = bf16[16,256,128]{2,1,0:T(8,128)(2,1)} collective-permute-done((bf16[16,256,128]{2,1,0:T(8,128)(2,1)S(1)}, bf16[16,256,128]{2,1,0:T(8,128)(2,1)}, u32[]{:S(2)}, u32[]{:S(2)}) %collective-permute-start.12) | collective-permute-done | bytes 1048608 | tf_op jit(solution)/shard_map/ppermute | solution.py:468
  58.3 4.9 %collective-permute-done.11.wb1 = bf16[16,256,128]{2,1,0:T(8,128)(2,1)} collective-permute-done((bf16[16,256,128]{2,1,0:T(8,128)(2,1)S(1)}, bf16[16,256,128]{2,1,0:T(8,128)(2,1)}, u32[]{:S(2)}, u32[]{:S(2)}) %collective-permute-start.11) | collective-permute-done | bytes 1048608 | tf_op jit(solution)/shard_map/ppermute | solution.py:468
  63.2 3.4 %collective-permute-start.13 = (bf16[16,256,128]{2,1,0:T(8,128)(2,1)}, bf16[16,256,128]{2,1,0:T(8,128)(2,1)S(1)}, u32[]{:S(2)}, u32[]{:S(2)}) collective-permute-start(bf16[16,256,128]{2,1,0:T(8,128)(2,1)} %collective-permute-done.11.wb1), channel_id=1, source_target_pairs={{0,4},{1,5},{2,6},{3,7},{4,8},{5,9},{6,10},{7,11},{8,12},{9,13},{1... | collective-permute-start | bytes 3145736 | tf_op jit(solution)/shard_map/ppermute | solution.py:473
  66.6 5.9 %collective-permute-start.14 = (bf16[16,256,128]{2,1,0:T(8,128)(2,1)}, bf16[16,256,128]{2,1,0:T(8,128)(2,1)S(1)}, u32[]{:S(2)}, u32[]{:S(2)}) collective-permute-start(bf16[16,256,128]{2,1,0:T(8,128)(2,1)} %collective-permute-done.12.wc1), channel_id=1, source_target_pairs={{0,1},{1,2},{2,3},{3,0},{4,5},{5,6},{6,7},{7,4},{8,9},{9,10},{10,1... | collective-permute-start | bytes 3145736 | tf_op jit(solution)/shard_map/ppermute | solution.py:473
  72.5 0.0 collective-permute-done.15.wb2
  72.5 10.9 %shard_map.98.before = f32[1024,512]{1,0:T(8,128)S(1)} custom-call(s32[2]{0:T(128)S(1)} %pad_add_fusion.place, bf16[512,8192]{1,0:T(8,128)(2,1)} %x0.3, bf16[512,8192]{1,0:T(8,128)(2,1)} %collective-permute-done.x1, bf16[16,256,128]{2,1,0:T(8,128)(2,1)} %collective-permute-done.11.wb1, bf16[16,256,128]{2,1,0:T(8,128)(2,1)} %collective-permute-done.12.wc1, ...), custom_call_target="tpu_custom_call" | custom-call | flops 4294967296 | bytes 20971520 | tf_op jit(solution)/shard_map/pallas_call | solution.py:341
  83.4 0.0 collective-permute-done.17.squares1
  83.4 0.0 collective-permute-done.13.wb
  83.4 1.1 collective-permute-done.14.wc
  84.6 5.0 %shard_map.99 = (bf16[512,1024]{1,0:T(8,128)(2,1)}, bf16[512,512]{1,0:T(8,128)(2,1)S(1)}, f32[32,128]{1,0:T(8,128)}) custom-call(s32[2]{0:T(128)S(1)} %pad_add_fusion.place, bf16[1024,4096]{1,0:T(8,128)(2,1)S(1)} %get-tuple-element.26.x, bf16[16,256,128]{2,1,0:T(8,128)(2,1)S(1)} %collective-permute-done.13.wb, ...), custom_call_target="tpu_custom_call" | custom-call | flops 2147483648 | bytes 12582912 | tf_op jit(solution)/shard_map/pallas_call | solution.py:394
  89.6 3.4 %collective-permute-start.18 = (bf16[512,512]{1,0:T(8,128)(2,1)S(1)}, bf16[512,512]{1,0:T(8,128)(2,1)S(1)}, u32[]{:S(2)}, u32[]{:S(2)}) collective-permute-start(bf16[512,512]{1,0:T(8,128)(2,1)S(1)} %get-tuple-element.35), channel_id=1, source_target_pairs={{0,64},{1,65},{2,66},{3,67},{4,68},{5,69},{6,70},{7,71},{8,72},{9,... | collective-permute-start | bytes 1572872 | tf_op jit(solution)/shard_map/ppermute | solution.py:478
  92.9 4.8 %all-to-all-start = ((f32[32,1,128]{2,1,0:T(1,128)}), f32[32,1,128]{2,1,0:T(1,128)S(1)}, u32[]{:S(2)}, u32[]{:S(2)}) async-start(f32[32,1,128]{2,1,0:T(1,128)} %bitcast.12), calls=%async_computation | async-start | bytes 32768 | tf_op jit(solution)/shard_map/all_to_all | solution.py:422
  97.7 6.7 %all-to-all-done = f32[32,1,128]{2,1,0:T(1,128)S(1)} async-done(((f32[32,1,128]{2,1,0:T(1,128)}), f32[32,1,128]{2,1,0:T(1,128)S(1)}, u32[]{:S(2)}, u32[]{:S(2)}) %all-to-all-start) | async-done | bytes 16416 | tf_op jit(solution)/shard_map/all_to_all | solution.py:422
  104.4 0.6 copy-done.3
  105.0 1.3 %shard_map.100 = f32[8,128]{1,0:T(8,128)} custom-call(f32[32,128]{1,0:T(8,128)} %bitcast.44), custom_call_target="tpu_custom_call" | custom-call | tf_op jit(solution)/shard_map/pallas_call | solution.py:482
  106.3 5.2 %all-to-all-start.1 = ((f32[8,1,128]{2,1,0:T(1,128)}), f32[8,1,128]{2,1,0:T(1,128)S(1)}, u32[]{:S(2)}, u32[]{:S(2)}) async-start(f32[8,1,128]{2,1,0:T(1,128)} %bitcast.45), calls=%async_computation.1 | async-start | bytes 8192 | tf_op jit(solution)/shard_map/all_to_all | solution.py:422
  111.5 0.0 collective-permute-done.18
  111.5 0.8 constant_dynamic-update-slice_fusion.14
  112.4 5.7 %all-to-all-done.1 = f32[8,1,128]{2,1,0:T(1,128)S(1)} async-done(((f32[8,1,128]{2,1,0:T(1,128)}), f32[8,1,128]{2,1,0:T(1,128)S(1)}, u32[]{:S(2)}, u32[]{:S(2)}) %all-to-all-start.1) | async-done | bytes 4128 | tf_op jit(solution)/shard_map/all_to_all | solution.py:422
  118.0 0.6 reduce_sum.9
  (25 shorter events, 0.4 us)
Async XLA Ops:
  0.6 44.2 %collective-permute-start = (bf16[512,8192]{1,0:T(8,128)(2,1)}, bf16[512,8192]{1,0:T(8,128)(2,1)}, u32[]{:S(2)}, u32[]{:S(2)}) collective-permute-start(bf16[512,8192]{1,0:T(8,128)(2,1)} %x0.3), channel_id=1, source_target_pairs={{0,64},{1,65},{2,66},{3,67},{4,68},{5,69},{6,70},{7,71},{8,72},{9,... | collective-permute-start | bytes 25165832 | tf_op jit(solution)/shard_map/ppermute | solution.py:443
  4.0 19.7 %collective-permute-start.1 = (bf16[512,1024]{1,0:T(8,128)(2,1)}, bf16[512,1024]{1,0:T(8,128)(2,1)S(1)}, u32[]{:S(2)}, u32[]{:S(2)}) collective-permute-start(bf16[512,1024]{1,0:T(8,128)(2,1)} %t0.1), channel_id=1, source_target_pairs={{0,64},{1,65},{2,66},{3,67},{4,68},{5,69},{6,70},{7,71},{8,72},{9,... | collective-permute-start | bytes 3145736 | tf_op jit(solution)/shard_map/ppermute | solution.py:445
  6.9 16.8 %copy-start.2 = (bf16[512,128]{1,0:T(8,128)(2,1)S(1)}, bf16[512,128]{1,0:T(8,128)(2,1)}, u32[]{:S(2)}) copy-start(bf16[512,128]{1,0:T(8,128)(2,1)} %shard_map.95) | copy-start | bytes 393220
  6.9 14.5 %collective-permute-start.2 = (bf16[512,128]{1,0:T(8,128)(2,1)}, bf16[512,128]{1,0:T(8,128)(2,1)S(1)}, u32[]{:S(2)}, u32[]{:S(2)}) collective-permute-start(bf16[512,128]{1,0:T(8,128)(2,1)} %shard_map.95), channel_id=1, source_target_pairs={{0,16},{1,17},{2,18},{3,19},{4,20},{5,21},{6,22},{7,23},{8,24},{9,... | collective-permute-start | bytes 393224 | tf_op jit(solution)/shard_map/ppermute | solution.py:68
  11.2 10.1 %collective-permute-start.3 = (bf16[512,128]{1,0:T(8,128)(2,1)}, bf16[512,128]{1,0:T(8,128)(2,1)S(1)}, u32[]{:S(2)}, u32[]{:S(2)}) collective-permute-start(bf16[512,128]{1,0:T(8,128)(2,1)} %shard_map.95), channel_id=1, source_target_pairs={{0,48},{1,49},{2,50},{3,51},{4,52},{5,53},{6,54},{7,55},{8,56},{9,... | collective-permute-start | bytes 393224 | tf_op jit(solution)/shard_map/ppermute | solution.py:69
  11.3 12.4 %collective-permute-start.4 = (bf16[512,128]{1,0:T(8,128)(2,1)}, bf16[512,128]{1,0:T(8,128)(2,1)S(1)}, u32[]{:S(2)}, u32[]{:S(2)}) collective-permute-start(bf16[512,128]{1,0:T(8,128)(2,1)} %shard_map.95), channel_id=1, source_target_pairs={{0,160},{1,161},{2,162},{3,163},{4,164},{5,165},{6,166},{7,167},{8... | collective-permute-start | bytes 393224 | tf_op jit(solution)/shard_map/ppermute | solution.py:71
  23.7 7.3 %collective-permute-start.8 = (bf16[4,256,128]{2,1,0:T(8,128)(2,1)S(1)}, bf16[4,256,128]{2,1,0:T(8,128)(2,1)S(1)}, u32[]{:S(2)}, u32[]{:S(2)}) collective-permute-start(bf16[4,256,128]{2,1,0:T(8,128)(2,1)S(1)} %pad_maximum_fusion.1), channel_id=1, source_target_pairs={{0,4},{1,5},{2,6},{3,7},{4,8},{5,9},{6,10},{7,11},{8,12},{9,13},{1... | collective-permute-start | bytes 786440 | tf_op jit(solution)/shard_map/ppermute | solution.py:68
  26.3 11.1 %collective-permute-start.9 = (bf16[4,256,128]{2,1,0:T(8,128)(2,1)S(1)}, bf16[4,256,128]{2,1,0:T(8,128)(2,1)S(1)}, u32[]{:S(2)}, u32[]{:S(2)}) collective-permute-start(bf16[4,256,128]{2,1,0:T(8,128)(2,1)S(1)} %pad_maximum_fusion.1), channel_id=1, source_target_pairs={{0,12},{1,13},{2,14},{3,15},{4,0},{5,1},{6,2},{7,3},{8,4},{9,5},{1... | collective-permute-start | bytes 786440 | tf_op jit(solution)/shard_map/ppermute | solution.py:69
  26.3 8.2 %collective-permute-start.5 = (bf16[4,256,128]{2,1,0:T(8,128)(2,1)S(1)}, bf16[4,256,128]{2,1,0:T(8,128)(2,1)S(1)}, u32[]{:S(2)}, u32[]{:S(2)}) collective-permute-start(bf16[4,256,128]{2,1,0:T(8,128)(2,1)S(1)} %pad_maximum_fusion), channel_id=1, source_target_pairs={{0,1},{1,2},{2,3},{3,0},{4,5},{5,6},{6,7},{7,4},{8,9},{9,10},{10,1... | collective-permute-start | bytes 786440 | tf_op jit(solution)/shard_map/ppermute | solution.py:68
  29.2 8.4 %collective-permute-start.6 = (bf16[4,256,128]{2,1,0:T(8,128)(2,1)S(1)}, bf16[4,256,128]{2,1,0:T(8,128)(2,1)S(1)}, u32[]{:S(2)}, u32[]{:S(2)}) collective-permute-start(bf16[4,256,128]{2,1,0:T(8,128)(2,1)S(1)} %pad_maximum_fusion), channel_id=1, source_target_pairs={{0,3},{1,0},{2,1},{3,2},{4,7},{5,4},{6,5},{7,6},{8,11},{9,8},{10,9... | collective-permute-start | bytes 786440 | tf_op jit(solution)/shard_map/ppermute | solution.py:69
  31.1 6.7 %collective-permute-start.10 = (bf16[4,256,128]{2,1,0:T(8,128)(2,1)S(1)}, bf16[4,256,128]{2,1,0:T(8,128)(2,1)S(1)}, u32[]{:S(2)}, u32[]{:S(2)}) collective-permute-start(bf16[4,256,128]{2,1,0:T(8,128)(2,1)S(1)} %collective-permute-done.8), channel_id=1, source_target_pairs={{0,4},{1,5},{2,6},{3,7},{4,8},{5,9},{6,10},{7,11},{8,12},{9,13},{1... | collective-permute-start | bytes 786440 | tf_op jit(solution)/shard_map/ppermute | solution.py:73
  34.5 6.1 %collective-permute-start.7 = (bf16[4,256,128]{2,1,0:T(8,128)(2,1)S(1)}, bf16[4,256,128]{2,1,0:T(8,128)(2,1)S(1)}, u32[]{:S(2)}, u32[]{:S(2)}) collective-permute-start(bf16[4,256,128]{2,1,0:T(8,128)(2,1)S(1)} %collective-permute-done.5), channel_id=1, source_target_pairs={{0,1},{1,2},{2,3},{3,0},{4,5},{5,6},{6,7},{7,4},{8,9},{9,10},{10,1... | collective-permute-start | bytes 786440 | tf_op jit(solution)/shard_map/ppermute | solution.py:73
  37.8 20.5 %collective-permute-start.12 = (bf16[16,256,128]{2,1,0:T(8,128)(2,1)S(1)}, bf16[16,256,128]{2,1,0:T(8,128)(2,1)}, u32[]{:S(2)}, u32[]{:S(2)}) collective-permute-start(bf16[16,256,128]{2,1,0:T(8,128)(2,1)S(1)} %constant_dynamic-update-slice_fusion.7.wc), channel_id=1, source_target_pairs={{0,1},{1,2},{2,3},{3,0},{4,5},{5,6},{6,7},{7,4},{8,9},{9,10},{10,1... | collective-permute-start | bytes 3145736 | tf_op jit(solution)/shard_map/ppermute | solution.py:468
  40.7 22.5 %collective-permute-start.11 = (bf16[16,256,128]{2,1,0:T(8,128)(2,1)S(1)}, bf16[16,256,128]{2,1,0:T(8,128)(2,1)}, u32[]{:S(2)}, u32[]{:S(2)}) collective-permute-start(bf16[16,256,128]{2,1,0:T(8,128)(2,1)S(1)} %constant_dynamic-update-slice_fusion.wb), channel_id=1, source_target_pairs={{0,4},{1,5},{2,6},{3,7},{4,8},{5,9},{6,10},{7,11},{8,12},{9,13},{1... | collective-permute-start | bytes 3145736 | tf_op jit(solution)/shard_map/ppermute | solution.py:468
  44.5 28.0 %copy-start = (f32[512,128]{1,0:T(8,128)S(1)}, f32[512,128]{1,0:T(8,128)}, u32[]{:S(2)}) copy-start(f32[512,128]{1,0:T(8,128)} %shard_map.96.squares0) | copy-start | bytes 786436
  44.5 28.0 %collective-permute-start.16 = (bf16[16,256,128]{2,1,0:T(8,128)(2,1)S(1)}, bf16[16,256,128]{2,1,0:T(8,128)(2,1)S(1)}, u32[]{:S(2)}, u32[]{:S(2)}) collective-permute-start(bf16[16,256,128]{2,1,0:T(8,128)(2,1)S(1)} %constant_dynamic-update-slice_fusion.7.wc), channel_id=1, source_target_pairs={{0,3},{1,0},{2,1},{3,2},{4,7},{5,4},{6,5},{7,6},{8,11},{9,8},{10,9... | collective-permute-start | bytes 3145736 | tf_op jit(solution)/shard_map/ppermute | solution.py:469
  44.6 28.0 %collective-permute-start.15 = (bf16[16,256,128]{2,1,0:T(8,128)(2,1)S(1)}, bf16[16,256,128]{2,1,0:T(8,128)(2,1)S(1)}, u32[]{:S(2)}, u32[]{:S(2)}) collective-permute-start(bf16[16,256,128]{2,1,0:T(8,128)(2,1)S(1)} %constant_dynamic-update-slice_fusion.wb), channel_id=1, source_target_pairs={{0,12},{1,13},{2,14},{3,15},{4,0},{5,1},{6,2},{7,3},{8,4},{9,5},{1... | collective-permute-start | bytes 3145736 | tf_op jit(solution)/shard_map/ppermute | solution.py:469
  63.2 21.4 %copy-start.1 = (bf16[512,1024]{1,0:T(8,128)(2,1)S(1)}, bf16[512,1024]{1,0:T(8,128)(2,1)}, u32[]{:S(2)}) copy-start(bf16[512,1024]{1,0:T(8,128)(2,1)} %t0.1) | copy-start | bytes 3145732
  63.2 20.2 %collective-permute-start.13 = (bf16[16,256,128]{2,1,0:T(8,128)(2,1)}, bf16[16,256,128]{2,1,0:T(8,128)(2,1)S(1)}, u32[]{:S(2)}, u32[]{:S(2)}) collective-permute-start(bf16[16,256,128]{2,1,0:T(8,128)(2,1)} %collective-permute-done.11.wb1), channel_id=1, source_target_pairs={{0,4},{1,5},{2,6},{3,7},{4,8},{5,9},{6,10},{7,11},{8,12},{9,13},{1... | collective-permute-start | bytes 3145736 | tf_op jit(solution)/shard_map/ppermute | solution.py:473
  66.6 18.0 %collective-permute-start.14 = (bf16[16,256,128]{2,1,0:T(8,128)(2,1)}, bf16[16,256,128]{2,1,0:T(8,128)(2,1)S(1)}, u32[]{:S(2)}, u32[]{:S(2)}) collective-permute-start(bf16[16,256,128]{2,1,0:T(8,128)(2,1)} %collective-permute-done.12.wc1), channel_id=1, source_target_pairs={{0,1},{1,2},{2,3},{3,0},{4,5},{5,6},{6,7},{7,4},{8,9},{9,10},{10,1... | collective-permute-start | bytes 3145736 | tf_op jit(solution)/shard_map/ppermute | solution.py:473
  72.5 10.9 %collective-permute-start.17 = (f32[512,128]{1,0:T(8,128)S(1)}, f32[512,128]{1,0:T(8,128)S(1)}, u32[]{:S(2)}, u32[]{:S(2)}) collective-permute-start(f32[512,128]{1,0:T(8,128)S(1)} %copy-done), channel_id=1, source_target_pairs={{0,64},{1,65},{2,66},{3,67},{4,68},{5,69},{6,70},{7,71},{8,72},{9,... | collective-permute-start | bytes 786440 | tf_op jit(solution)/shard_map/ppermute | solution.py:461
  89.6 22.0 %collective-permute-start.18 = (bf16[512,512]{1,0:T(8,128)(2,1)S(1)}, bf16[512,512]{1,0:T(8,128)(2,1)S(1)}, u32[]{:S(2)}, u32[]{:S(2)}) collective-permute-start(bf16[512,512]{1,0:T(8,128)(2,1)S(1)} %get-tuple-element.35), channel_id=1, source_target_pairs={{0,64},{1,65},{2,66},{3,67},{4,68},{5,69},{6,70},{7,71},{8,72},{9,... | collective-permute-start | bytes 1572872 | tf_op jit(solution)/shard_map/ppermute | solution.py:478
  92.9 11.5 %all-to-all-start = ((f32[32,1,128]{2,1,0:T(1,128)}), f32[32,1,128]{2,1,0:T(1,128)S(1)}, u32[]{:S(2)}, u32[]{:S(2)}) async-start(f32[32,1,128]{2,1,0:T(1,128)} %bitcast.12), calls=%async_computation | async-start | bytes 32768 | tf_op jit(solution)/shard_map/all_to_all | solution.py:422
  104.4 0.6 copy-start.3
  106.3 11.7 %all-to-all-start.1 = ((f32[8,1,128]{2,1,0:T(1,128)}), f32[8,1,128]{2,1,0:T(1,128)S(1)}, u32[]{:S(2)}, u32[]{:S(2)}) async-start(f32[8,1,128]{2,1,0:T(1,128)} %bitcast.45), calls=%async_computation.1 | async-start | bytes 8192 | tf_op jit(solution)/shard_map/all_to_all | solution.py:422

commit v4 on v3

--- a/solution.py
+++ b/solution.py
@@ -455,10 +455,8 @@
     own_rows, own_weight = lax.optimization_barrier((layer_input_rows, own_weight))
     own_squares = sum_squares(own_rows)
     along_z = ring(own_weight, ZH)
-    own_squares, other_target, *along_z = lax.optimization_barrier(
-        (own_squares, other_target, *along_z)
-    )
-    squares = (own_squares, lax.ppermute(own_squares, AXES, OTHER_CORE))
+    own_squares, *along_z = lax.optimization_barrier((own_squares, *along_z))
+    other_squares = lax.ppermute(own_squares, AXES, OTHER_CORE)
     planes = []
     for part, (middle, last) in enumerate(ORDER):
         columns = slice(part * PART, (part + 1) * PART)
@@ -467,7 +465,9 @@
 
     behind = [lax.ppermute(p, AXES, FORWARD[last]) for p, (_, last) in zip(planes, ORDER)]
     ahead = [lax.ppermute(p, AXES, BACKWARD[last]) for p, (_, last) in zip(planes, ORDER)]
-    x = (layer_input_rows, other_rows)
+    own_rows, other_squares = lax.optimization_barrier((layer_input_rows, other_squares))
+    squares = (own_squares, other_squares)
+    x = (own_rows, other_rows)
     total, last_x = first(place, x, planes)
     total, *behind = lax.optimization_barrier((total, *behind))
     opposite = [lax.ppermute(p, AXES, FORWARD[last]) for p, (_, last) in zip(behind, ORDER)]

time: 121 us -> 122 us (level)
  waiting for transfers between devices: 26.8 us -> 22.9 us
  starting transfers between devices: 51.7 us -> 55.5 us
    ppermute x4, waiting for transfers between devices: 10 us -> 4.58 us  [per_device(): lax.ppermute(p, AXES, FORWARD[last])]
    all_to_all x2, starting transfers between devices: 9.97 us -> 11.7 us  [swap_rows(): lax.all_to_all(everyone, AXES, 0, 0, axis_index_groups=groups, tiled=True)]
    ppermute x2, starting transfers between devices: 0.28 us -> 1.59 us  [per_device(): lax.ppermute(p, AXES, BACKWARD[last])]
  transfers between devices with their start and end apart: 21 -> 21, of which waited for: 9 -> 10; matrix products, arithmetic and copies ran while one was open for 1% -> 1% of each run, Pallas kernels for 26% -> 26%
where the time goes in v4:
time: 122 us; the launch traced here: 121 us
  starting transfers between devices  55.5 us (45%)
  Pallas kernels  37.6 us (31%)
  waiting for transfers between devices  22.9 us (19%)
  between operations  2.6 us (2%)
  local copies, waits for them, and re-layouts  1.77 us (1%)
    ppermute x4, starting transfers between devices, per_device(): lax.ppermute(p, AXES, FORWARD[last])  15.5 us
    all_to_all x2, waiting for transfers between devices, swap_rows(): lax.all_to_all(everyone, AXES, 0, 0, axis_index_groups=groups, tiled=True)  12.4 us
    all_to_all x2, starting transfers between devices, swap_rows(): lax.all_to_all(everyone, AXES, 0, 0, axis_index_groups=groups, tiled=True)  11.7 us
    pallas_call x1, Pallas kernels, following(): pl.pallas_call(next_kernel, grid_spec=pltpu.PrefetchScalarGridSpec(num_sc...  10.9 us
    ppermute x3, starting transfers between devices, ring(): behind = lax.ppermute(block, AXES, FORWARD[axis])  9.72 us
    pallas_call x1, Pallas kernels, first(): pl.pallas_call(first_kernel, grid_spec=pltpu.PrefetchScalarGridSpec(num_s...  9.48 us
    pallas_call x1, Pallas kernels, sum_squares(): pl.pallas_call(squares_kernel, grid=(8,), in_specs=[pl.BlockSpec((tokens...  7.32 us
    ppermute x2, starting transfers between devices, ring(): opposite = lax.ppermute(behind, AXES, FORWARD[axis])  6.22 us
  transfers between devices with their start and end apart: 21, of which 10 were waited for; matrix products, arithmetic and copies ran while one was open for 1% of the time, Pallas kernels for 26%

profile of v4, /device:TPU:1, one launch (start us, length us, event | category | flops | bytes accessed | tf_op | source)
XLA Modules:
  0.0 121.1 jit_solution(6119565750163602740)
XLA Ops:
  0.6 3.3 %collective-permute-start.4 = (bf16[512,8192]{1,0:T(8,128)(2,1)}, bf16[512,8192]{1,0:T(8,128)(2,1)}, u32[]{:S(2)}, u32[]{:S(2)}) collective-permute-start(bf16[512,8192]{1,0:T(8,128)(2,1)} %x0.1), channel_id=1, source_target_pairs={{0,64},{1,65},{2,66},{3,67},{4,68},{5,69},{6,70},{7,71},{8,72},{9,... | collective-permute-start | bytes 25165832 | tf_op jit(solution)/shard_map/ppermute | solution.py:443
  4.0 2.8 %shard_map.95 = bf16[512,128]{1,0:T(8,128)(2,1)} custom-call(s32[8]{0:T(128)} %outer.1, s32[128,256]{1,0:T(8,128)} %words.1, s32[4,128]{1,0:T(4,128)} %scale_words.1, bf16[8192]{0:T(1024)(128)(2,1)} %gain.1, bf16[64,8192]{1,0:T(8,128)(2,1)} %bitcast.43, bf16[64,1024]{1,0:T(8,128)(2,1)} %up.1), custom_call_target="tpu_custom_call" | custom-call | tf_op jit(solution)/shard_map/pallas_call | solution.py:160
  6.8 4.4 %collective-permute-start = (bf16[512,128]{1,0:T(8,128)(2,1)}, bf16[512,128]{1,0:T(8,128)(2,1)S(1)}, u32[]{:S(2)}, u32[]{:S(2)}) collective-permute-start(bf16[512,128]{1,0:T(8,128)(2,1)} %shard_map.95), channel_id=1, source_target_pairs={{0,16},{1,17},{2,18},{3,19},{4,20},{5,21},{6,22},{7,23},{8,24},{9,... | collective-permute-start | bytes 393224 | tf_op jit(solution)/shard_map/ppermute | solution.py:68
  11.2 0.0 collective-permute-start.1
  11.2 2.8 %collective-permute-start.2 = (bf16[512,128]{1,0:T(8,128)(2,1)}, bf16[512,128]{1,0:T(8,128)(2,1)S(1)}, u32[]{:S(2)}, u32[]{:S(2)}) collective-permute-start(bf16[512,128]{1,0:T(8,128)(2,1)} %shard_map.95), channel_id=1, source_target_pairs={{0,160},{1,161},{2,162},{3,163},{4,164},{5,165},{6,166},{7,167},{8... | collective-permute-start | bytes 393224 | tf_op jit(solution)/shard_map/ppermute | solution.py:71
  14.0 7.3 %shard_map.96.squares0 = f32[512,128]{1,0:T(8,128)} custom-call(bf16[512,8192]{1,0:T(8,128)(2,1)} %x0.1), custom_call_target="tpu_custom_call" | custom-call | tf_op jit(solution)/shard_map/pallas_call | solution.py:285
  21.3 0.0 collective-permute-done
  21.3 0.0 collective-permute-done.1
  21.3 1.9 %collective-permute-done.2 = bf16[512,128]{1,0:T(8,128)(2,1)S(1)} collective-permute-done((bf16[512,128]{1,0:T(8,128)(2,1)}, bf16[512,128]{1,0:T(8,128)(2,1)S(1)}, u32[]{:S(2)}, u32[]{:S(2)}) %collective-permute-start.2) | collective-permute-done | bytes 131104 | tf_op jit(solution)/shard_map/ppermute | solution.py:71
  23.3 2.5 %collective-permute-start.8 = (bf16[4,256,128]{2,1,0:T(8,128)(2,1)S(1)}, bf16[4,256,128]{2,1,0:T(8,128)(2,1)S(1)}, u32[]{:S(2)}, u32[]{:S(2)}) collective-permute-start(bf16[4,256,128]{2,1,0:T(8,128)(2,1)S(1)} %pad_maximum_fusion.1), channel_id=1, source_target_pairs={{0,4},{1,5},{2,6},{3,7},{4,8},{5,9},{6,10},{7,11},{8,12},{9,13},{1... | collective-permute-start | bytes 786440 | tf_op jit(solution)/shard_map/ppermute | solution.py:68
  25.8 0.0 collective-permute-start.9
  25.9 2.8 %collective-permute-start.5 = (bf16[4,256,128]{2,1,0:T(8,128)(2,1)S(1)}, bf16[4,256,128]{2,1,0:T(8,128)(2,1)S(1)}, u32[]{:S(2)}, u32[]{:S(2)}) collective-permute-start(bf16[4,256,128]{2,1,0:T(8,128)(2,1)S(1)} %pad_maximum_fusion), channel_id=1, source_target_pairs={{0,1},{1,2},{2,3},{3,0},{4,5},{5,6},{6,7},{7,4},{8,9},{9,10},{10,1... | collective-permute-start | bytes 786440 | tf_op jit(solution)/shard_map/ppermute | solution.py:68
  28.7 0.0 collective-permute-start.6
  28.8 1.8 %collective-permute-done.8 = bf16[4,256,128]{2,1,0:T(8,128)(2,1)S(1)} collective-permute-done((bf16[4,256,128]{2,1,0:T(8,128)(2,1)S(1)}, bf16[4,256,128]{2,1,0:T(8,128)(2,1)S(1)}, u32[]{:S(2)}, u32[]{:S(2)}) %collective-permute-start.8) | collective-permute-done | bytes 262176 | tf_op jit(solution)/shard_map/ppermute | solution.py:68
  30.5 3.4 %collective-permute-start.10 = (bf16[4,256,128]{2,1,0:T(8,128)(2,1)S(1)}, bf16[4,256,128]{2,1,0:T(8,128)(2,1)S(1)}, u32[]{:S(2)}, u32[]{:S(2)}) collective-permute-start(bf16[4,256,128]{2,1,0:T(8,128)(2,1)S(1)} %collective-permute-done.8), channel_id=1, source_target_pairs={{0,4},{1,5},{2,6},{3,7},{4,8},{5,9},{6,10},{7,11},{8,12},{9,13},{1... | collective-permute-start | bytes 786440 | tf_op jit(solution)/shard_map/ppermute | solution.py:73
  34.0 0.0 collective-permute-done.5
  34.0 2.8 %collective-permute-start.7 = (bf16[4,256,128]{2,1,0:T(8,128)(2,1)S(1)}, bf16[4,256,128]{2,1,0:T(8,128)(2,1)S(1)}, u32[]{:S(2)}, u32[]{:S(2)}) collective-permute-start(bf16[4,256,128]{2,1,0:T(8,128)(2,1)S(1)} %collective-permute-done.5), channel_id=1, source_target_pairs={{0,1},{1,2},{2,3},{3,0},{4,5},{5,6},{6,7},{7,4},{8,9},{9,10},{10,1... | collective-permute-start | bytes 786440 | tf_op jit(solution)/shard_map/ppermute | solution.py:73
  36.8 0.0 collective-permute-done.9
  36.9 0.2 collective-permute-done.6
  37.2 0.1 collective-permute-done.10
  37.3 2.8 %collective-permute-start.12 = (bf16[16,256,128]{2,1,0:T(8,128)(2,1)S(1)}, bf16[16,256,128]{2,1,0:T(8,128)(2,1)}, u32[]{:S(2)}, u32[]{:S(2)}) collective-permute-start(bf16[16,256,128]{2,1,0:T(8,128)(2,1)S(1)} %constant_dynamic-update-slice_fusion.7.wc), channel_id=1, source_target_pairs={{0,1},{1,2},{2,3},{3,0},{4,5},{5,6},{6,7},{7,4},{8,9},{9,10},{10,1... | collective-permute-start | bytes 3145736 | tf_op jit(solution)/shard_map/ppermute | solution.py:466
  40.1 0.0 collective-permute-done.7
  40.2 3.8 %collective-permute-start.11 = (bf16[16,256,128]{2,1,0:T(8,128)(2,1)S(1)}, bf16[16,256,128]{2,1,0:T(8,128)(2,1)}, u32[]{:S(2)}, u32[]{:S(2)}) collective-permute-start(bf16[16,256,128]{2,1,0:T(8,128)(2,1)S(1)} %constant_dynamic-update-slice_fusion.wb), channel_id=1, source_target_pairs={{0,4},{1,5},{2,6},{3,7},{4,8},{5,9},{6,10},{7,11},{8,12},{9,13},{1... | collective-permute-start | bytes 3145736 | tf_op jit(solution)/shard_map/ppermute | solution.py:466
  43.9 0.3 collective-permute-start.3
  44.2 0.2 collective-permute-start.17
  44.5 0.1 pad_add_fusion.place
  44.5 1.2 collective-permute-done.3.squares1
  45.7 0.4 collective-permute-start.16
  46.1 1.2 %collective-permute-start.15 = (bf16[16,256,128]{2,1,0:T(8,128)(2,1)S(1)}, bf16[16,256,128]{2,1,0:T(8,128)(2,1)S(1)}, u32[]{:S(2)}, u32[]{:S(2)}) collective-permute-start(bf16[16,256,128]{2,1,0:T(8,128)(2,1)S(1)} %constant_dynamic-update-slice_fusion.wb), channel_id=1, source_target_pairs={{0,12},{1,13},{2,14},{3,15},{4,0},{5,1},{6,2},{7,3},{8,4},{9,5},{1... | collective-permute-start | bytes 3145736 | tf_op jit(solution)/shard_map/ppermute | solution.py:467
  47.3 9.5 %shard_map.97 = (f32[1024,512]{1,0:T(8,128)S(1)}, bf16[1024,4096]{1,0:T(8,128)(2,1)S(1)}) custom-call(s32[2]{0:T(128)S(1)} %pad_add_fusion.place, bf16[512,8192]{1,0:T(8,128)(2,1)} %x0.1, bf16[512,8192]{1,0:T(8,128)(2,1)} %collective-permute-done.4.x1, bf16[16,256,128]{2,1,0:T(8,128)(2,1)S(1)} %constant_dynamic-update-slice_fusion.wb, ...), custom_call_target="tpu_custom_call" | custom-call | flops 4294967296 | bytes 20971520 | tf_op jit(solution)/shard_map/pallas_call | solution.py:307
  56.8 0.0 collective-permute-done.12.wc1
  56.8 4.2 %collective-permute-done.11.wb1 = bf16[16,256,128]{2,1,0:T(8,128)(2,1)} collective-permute-done((bf16[16,256,128]{2,1,0:T(8,128)(2,1)S(1)}, bf16[16,256,128]{2,1,0:T(8,128)(2,1)}, u32[]{:S(2)}, u32[]{:S(2)}) %collective-permute-start.11) | collective-permute-done | bytes 1048608 | tf_op jit(solution)/shard_map/ppermute | solution.py:466
  61.0 3.4 %collective-permute-start.13 = (bf16[16,256,128]{2,1,0:T(8,128)(2,1)}, bf16[16,256,128]{2,1,0:T(8,128)(2,1)S(1)}, u32[]{:S(2)}, u32[]{:S(2)}) collective-permute-start(bf16[16,256,128]{2,1,0:T(8,128)(2,1)} %collective-permute-done.11.wb1), channel_id=1, source_target_pairs={{0,4},{1,5},{2,6},{3,7},{4,8},{5,9},{6,10},{7,11},{8,12},{9,13},{1... | collective-permute-start | bytes 3145736 | tf_op jit(solution)/shard_map/ppermute | solution.py:473
  64.4 5.5 %collective-permute-start.14 = (bf16[16,256,128]{2,1,0:T(8,128)(2,1)}, bf16[16,256,128]{2,1,0:T(8,128)(2,1)S(1)}, u32[]{:S(2)}, u32[]{:S(2)}) collective-permute-start(bf16[16,256,128]{2,1,0:T(8,128)(2,1)} %collective-permute-done.12.wc1), channel_id=1, source_target_pairs={{0,1},{1,2},{2,3},{3,0},{4,5},{5,6},{6,7},{7,4},{8,9},{9,10},{10,1... | collective-permute-start | bytes 3145736 | tf_op jit(solution)/shard_map/ppermute | solution.py:473
  69.9 0.0 collective-permute-done.16.wc2
  69.9 0.8 collective-permute-done.15.wb2
  70.7 10.9 %shard_map.98.before = f32[1024,512]{1,0:T(8,128)S(1)} custom-call(s32[2]{0:T(128)S(1)} %pad_add_fusion.place, bf16[512,8192]{1,0:T(8,128)(2,1)} %x0.1, bf16[512,8192]{1,0:T(8,128)(2,1)} %collective-permute-done.4.x1, bf16[16,256,128]{2,1,0:T(8,128)(2,1)} %collective-permute-done.11.wb1, bf16[16,256,128]{2,1,0:T(8,128)(2,1)} %collective-permute-done.12.wc1, ...), custom_call_target="tpu_custom_call" | custom-call | flops 4294967296 | bytes 20971520 | tf_op jit(solution)/shard_map/pallas_call | solution.py:341
  81.6 0.4 collective-permute-done.14.wc
  81.9 5.8 %shard_map.99 = (bf16[512,1024]{1,0:T(8,128)(2,1)}, bf16[512,512]{1,0:T(8,128)(2,1)S(1)}, f32[32,128]{1,0:T(8,128)}) custom-call(s32[2]{0:T(128)S(1)} %pad_add_fusion.place, bf16[1024,4096]{1,0:T(8,128)(2,1)S(1)} %get-tuple-element.29.x, bf16[16,256,128]{2,1,0:T(8,128)(2,1)S(1)} %collective-permute-done.13.wb, ...), custom_call_target="tpu_custom_call" | custom-call | flops 2147483648 | bytes 12582912 | tf_op jit(solution)/shard_map/pallas_call | solution.py:394
  87.7 4.2 %collective-permute-start.18 = (bf16[512,512]{1,0:T(8,128)(2,1)S(1)}, bf16[512,512]{1,0:T(8,128)(2,1)S(1)}, u32[]{:S(2)}, u32[]{:S(2)}) collective-permute-start(bf16[512,512]{1,0:T(8,128)(2,1)S(1)} %get-tuple-element.37), channel_id=1, source_target_pairs={{0,64},{1,65},{2,66},{3,67},{4,68},{5,69},{6,70},{7,71},{8,72},{9,... | collective-permute-start | bytes 1572872 | tf_op jit(solution)/shard_map/ppermute | solution.py:478
  91.9 4.8 %all-to-all-start = ((f32[32,1,128]{2,1,0:T(1,128)}), f32[32,1,128]{2,1,0:T(1,128)S(1)}, u32[]{:S(2)}, u32[]{:S(2)}) async-start(f32[32,1,128]{2,1,0:T(1,128)} %bitcast.12), calls=%async_computation | async-start | bytes 32768 | tf_op jit(solution)/shard_map/all_to_all | solution.py:422
  96.7 6.7 %all-to-all-done = f32[32,1,128]{2,1,0:T(1,128)S(1)} async-done(((f32[32,1,128]{2,1,0:T(1,128)}), f32[32,1,128]{2,1,0:T(1,128)S(1)}, u32[]{:S(2)}, u32[]{:S(2)}) %all-to-all-start) | async-done | bytes 16416 | tf_op jit(solution)/shard_map/all_to_all | solution.py:422
  103.4 0.6 copy-done.3
  104.0 1.3 %shard_map.100 = f32[8,128]{1,0:T(8,128)} custom-call(f32[32,128]{1,0:T(8,128)} %bitcast.44), custom_call_target="tpu_custom_call" | custom-call | tf_op jit(solution)/shard_map/pallas_call | solution.py:482
  105.3 6.9 %all-to-all-start.1 = ((f32[8,1,128]{2,1,0:T(1,128)}), f32[8,1,128]{2,1,0:T(1,128)S(1)}, u32[]{:S(2)}, u32[]{:S(2)}) async-start(f32[8,1,128]{2,1,0:T(1,128)} %bitcast.45), calls=%async_computation.1 | async-start | bytes 8192 | tf_op jit(solution)/shard_map/all_to_all | solution.py:422
  112.2 0.8 constant_dynamic-update-slice_fusion.14
  113.1 5.7 %all-to-all-done.1 = f32[8,1,128]{2,1,0:T(1,128)S(1)} async-done(((f32[8,1,128]{2,1,0:T(1,128)}), f32[8,1,128]{2,1,0:T(1,128)S(1)}, u32[]{:S(2)}, u32[]{:S(2)}) %all-to-all-start.1) | async-done | bytes 4128 | tf_op jit(solution)/shard_map/all_to_all | solution.py:422
  118.7 0.6 reduce_sum.9
  (25 shorter events, 0.4 us)
Async XLA Ops:
  0.6 43.6 %copy-start.1 = (bf16[512,1024]{1,0:T(8,128)(2,1)S(1)}, bf16[512,1024]{1,0:T(8,128)(2,1)}, u32[]{:S(2)}) copy-start(bf16[512,1024]{1,0:T(8,128)(2,1)} %t0.1) | copy-start | bytes 3145732
  0.6 45.4 %collective-permute-start.4 = (bf16[512,8192]{1,0:T(8,128)(2,1)}, bf16[512,8192]{1,0:T(8,128)(2,1)}, u32[]{:S(2)}, u32[]{:S(2)}) collective-permute-start(bf16[512,8192]{1,0:T(8,128)(2,1)} %x0.1), channel_id=1, source_target_pairs={{0,64},{1,65},{2,66},{3,67},{4,68},{5,69},{6,70},{7,71},{8,72},{9,... | collective-permute-start | bytes 25165832 | tf_op jit(solution)/shard_map/ppermute | solution.py:443
  6.8 16.4 %copy-start.2 = (bf16[512,128]{1,0:T(8,128)(2,1)S(1)}, bf16[512,128]{1,0:T(8,128)(2,1)}, u32[]{:S(2)}) copy-start(bf16[512,128]{1,0:T(8,128)(2,1)} %shard_map.95) | copy-start | bytes 393220
  6.8 14.5 %collective-permute-start = (bf16[512,128]{1,0:T(8,128)(2,1)}, bf16[512,128]{1,0:T(8,128)(2,1)S(1)}, u32[]{:S(2)}, u32[]{:S(2)}) collective-permute-start(bf16[512,128]{1,0:T(8,128)(2,1)} %shard_map.95), channel_id=1, source_target_pairs={{0,16},{1,17},{2,18},{3,19},{4,20},{5,21},{6,22},{7,23},{8,24},{9,... | collective-permute-start | bytes 393224 | tf_op jit(solution)/shard_map/ppermute | solution.py:68
  11.2 10.1 %collective-permute-start.1 = (bf16[512,128]{1,0:T(8,128)(2,1)}, bf16[512,128]{1,0:T(8,128)(2,1)S(1)}, u32[]{:S(2)}, u32[]{:S(2)}) collective-permute-start(bf16[512,128]{1,0:T(8,128)(2,1)} %shard_map.95), channel_id=1, source_target_pairs={{0,48},{1,49},{2,50},{3,51},{4,52},{5,53},{6,54},{7,55},{8,56},{9,... | collective-permute-start | bytes 393224 | tf_op jit(solution)/shard_map/ppermute | solution.py:69
  11.2 12.0 %collective-permute-start.2 = (bf16[512,128]{1,0:T(8,128)(2,1)}, bf16[512,128]{1,0:T(8,128)(2,1)S(1)}, u32[]{:S(2)}, u32[]{:S(2)}) collective-permute-start(bf16[512,128]{1,0:T(8,128)(2,1)} %shard_map.95), channel_id=1, source_target_pairs={{0,160},{1,161},{2,162},{3,163},{4,164},{5,165},{6,166},{7,167},{8... | collective-permute-start | bytes 393224 | tf_op jit(solution)/shard_map/ppermute | solution.py:71
  23.3 7.3 %collective-permute-start.8 = (bf16[4,256,128]{2,1,0:T(8,128)(2,1)S(1)}, bf16[4,256,128]{2,1,0:T(8,128)(2,1)S(1)}, u32[]{:S(2)}, u32[]{:S(2)}) collective-permute-start(bf16[4,256,128]{2,1,0:T(8,128)(2,1)S(1)} %pad_maximum_fusion.1), channel_id=1, source_target_pairs={{0,4},{1,5},{2,6},{3,7},{4,8},{5,9},{6,10},{7,11},{8,12},{9,13},{1... | collective-permute-start | bytes 786440 | tf_op jit(solution)/shard_map/ppermute | solution.py:68
  25.8 11.0 %collective-permute-start.9 = (bf16[4,256,128]{2,1,0:T(8,128)(2,1)S(1)}, bf16[4,256,128]{2,1,0:T(8,128)(2,1)S(1)}, u32[]{:S(2)}, u32[]{:S(2)}) collective-permute-start(bf16[4,256,128]{2,1,0:T(8,128)(2,1)S(1)} %pad_maximum_fusion.1), channel_id=1, source_target_pairs={{0,12},{1,13},{2,14},{3,15},{4,0},{5,1},{6,2},{7,3},{8,4},{9,5},{1... | collective-permute-start | bytes 786440 | tf_op jit(solution)/shard_map/ppermute | solution.py:69
  25.9 8.1 %collective-permute-start.5 = (bf16[4,256,128]{2,1,0:T(8,128)(2,1)S(1)}, bf16[4,256,128]{2,1,0:T(8,128)(2,1)S(1)}, u32[]{:S(2)}, u32[]{:S(2)}) collective-permute-start(bf16[4,256,128]{2,1,0:T(8,128)(2,1)S(1)} %pad_maximum_fusion), channel_id=1, source_target_pairs={{0,1},{1,2},{2,3},{3,0},{4,5},{5,6},{6,7},{7,4},{8,9},{9,10},{10,1... | collective-permute-start | bytes 786440 | tf_op jit(solution)/shard_map/ppermute | solution.py:68
  28.7 8.4 %collective-permute-start.6 = (bf16[4,256,128]{2,1,0:T(8,128)(2,1)S(1)}, bf16[4,256,128]{2,1,0:T(8,128)(2,1)S(1)}, u32[]{:S(2)}, u32[]{:S(2)}) collective-permute-start(bf16[4,256,128]{2,1,0:T(8,128)(2,1)S(1)} %pad_maximum_fusion), channel_id=1, source_target_pairs={{0,3},{1,0},{2,1},{3,2},{4,7},{5,4},{6,5},{7,6},{8,11},{9,8},{10,9... | collective-permute-start | bytes 786440 | tf_op jit(solution)/shard_map/ppermute | solution.py:69
  30.5 6.7 %collective-permute-start.10 = (bf16[4,256,128]{2,1,0:T(8,128)(2,1)S(1)}, bf16[4,256,128]{2,1,0:T(8,128)(2,1)S(1)}, u32[]{:S(2)}, u32[]{:S(2)}) collective-permute-start(bf16[4,256,128]{2,1,0:T(8,128)(2,1)S(1)} %collective-permute-done.8), channel_id=1, source_target_pairs={{0,4},{1,5},{2,6},{3,7},{4,8},{5,9},{6,10},{7,11},{8,12},{9,13},{1... | collective-permute-start | bytes 786440 | tf_op jit(solution)/shard_map/ppermute | solution.py:73
  34.0 6.1 %collective-permute-start.7 = (bf16[4,256,128]{2,1,0:T(8,128)(2,1)S(1)}, bf16[4,256,128]{2,1,0:T(8,128)(2,1)S(1)}, u32[]{:S(2)}, u32[]{:S(2)}) collective-permute-start(bf16[4,256,128]{2,1,0:T(8,128)(2,1)S(1)} %collective-permute-done.5), channel_id=1, source_target_pairs={{0,1},{1,2},{2,3},{3,0},{4,5},{5,6},{6,7},{7,4},{8,9},{9,10},{10,1... | collective-permute-start | bytes 786440 | tf_op jit(solution)/shard_map/ppermute | solution.py:73
  37.3 19.5 %collective-permute-start.12 = (bf16[16,256,128]{2,1,0:T(8,128)(2,1)S(1)}, bf16[16,256,128]{2,1,0:T(8,128)(2,1)}, u32[]{:S(2)}, u32[]{:S(2)}) collective-permute-start(bf16[16,256,128]{2,1,0:T(8,128)(2,1)S(1)} %constant_dynamic-update-slice_fusion.7.wc), channel_id=1, source_target_pairs={{0,1},{1,2},{2,3},{3,0},{4,5},{5,6},{6,7},{7,4},{8,9},{9,10},{10,1... | collective-permute-start | bytes 3145736 | tf_op jit(solution)/shard_map/ppermute | solution.py:466
  40.2 20.8 %collective-permute-start.11 = (bf16[16,256,128]{2,1,0:T(8,128)(2,1)S(1)}, bf16[16,256,128]{2,1,0:T(8,128)(2,1)}, u32[]{:S(2)}, u32[]{:S(2)}) collective-permute-start(bf16[16,256,128]{2,1,0:T(8,128)(2,1)S(1)} %constant_dynamic-update-slice_fusion.wb), channel_id=1, source_target_pairs={{0,4},{1,5},{2,6},{3,7},{4,8},{5,9},{6,10},{7,11},{8,12},{9,13},{1... | collective-permute-start | bytes 3145736 | tf_op jit(solution)/shard_map/ppermute | solution.py:466
  43.9 1.7 %collective-permute-start.3 = (f32[512,128]{1,0:T(8,128)}, f32[512,128]{1,0:T(8,128)S(1)}, u32[]{:S(2)}, u32[]{:S(2)}) collective-permute-start(f32[512,128]{1,0:T(8,128)} %shard_map.96.squares0), channel_id=1, source_target_pairs={{0,64},{1,65},{2,66},{3,67},{4,68},{5,69},{6,70},{7,71},{8,72},{9,... | collective-permute-start | bytes 786440 | tf_op jit(solution)/shard_map/ppermute | solution.py:459
  44.2 37.3 %collective-permute-start.17 = (bf16[512,1024]{1,0:T(8,128)(2,1)S(1)}, bf16[512,1024]{1,0:T(8,128)(2,1)}, u32[]{:S(2)}, u32[]{:S(2)}) collective-permute-start(bf16[512,1024]{1,0:T(8,128)(2,1)S(1)} %copy-done.1), channel_id=1, source_target_pairs={{0,64},{1,65},{2,66},{3,67},{4,68},{5,69},{6,70},{7,71},{8,72},{9,... | collective-permute-start | bytes 3145736 | tf_op jit(solution)/shard_map/ppermute | solution.py:445
  45.7 24.2 %collective-permute-start.16 = (bf16[16,256,128]{2,1,0:T(8,128)(2,1)S(1)}, bf16[16,256,128]{2,1,0:T(8,128)(2,1)S(1)}, u32[]{:S(2)}, u32[]{:S(2)}) collective-permute-start(bf16[16,256,128]{2,1,0:T(8,128)(2,1)S(1)} %constant_dynamic-update-slice_fusion.7.wc), channel_id=1, source_target_pairs={{0,3},{1,0},{2,1},{3,2},{4,7},{5,4},{6,5},{7,6},{8,11},{9,8},{10,9... | collective-permute-start | bytes 3145736 | tf_op jit(solution)/shard_map/ppermute | solution.py:467
  46.1 24.6 %collective-permute-start.15 = (bf16[16,256,128]{2,1,0:T(8,128)(2,1)S(1)}, bf16[16,256,128]{2,1,0:T(8,128)(2,1)S(1)}, u32[]{:S(2)}, u32[]{:S(2)}) collective-permute-start(bf16[16,256,128]{2,1,0:T(8,128)(2,1)S(1)} %constant_dynamic-update-slice_fusion.wb), channel_id=1, source_target_pairs={{0,12},{1,13},{2,14},{3,15},{4,0},{5,1},{6,2},{7,3},{8,4},{9,5},{1... | collective-permute-start | bytes 3145736 | tf_op jit(solution)/shard_map/ppermute | solution.py:467
  61.0 20.9 %copy-start = (f32[512,128]{1,0:T(8,128)S(1)}, f32[512,128]{1,0:T(8,128)}, u32[]{:S(2)}) copy-start(f32[512,128]{1,0:T(8,128)} %shard_map.96.squares0) | copy-start | bytes 786436
  61.0 20.6 %collective-permute-start.13 = (bf16[16,256,128]{2,1,0:T(8,128)(2,1)}, bf16[16,256,128]{2,1,0:T(8,128)(2,1)S(1)}, u32[]{:S(2)}, u32[]{:S(2)}) collective-permute-start(bf16[16,256,128]{2,1,0:T(8,128)(2,1)} %collective-permute-done.11.wb1), channel_id=1, source_target_pairs={{0,4},{1,5},{2,6},{3,7},{4,8},{5,9},{6,10},{7,11},{8,12},{9,13},{1... | collective-permute-start | bytes 3145736 | tf_op jit(solution)/shard_map/ppermute | solution.py:473
  64.4 17.5 %collective-permute-start.14 = (bf16[16,256,128]{2,1,0:T(8,128)(2,1)}, bf16[16,256,128]{2,1,0:T(8,128)(2,1)S(1)}, u32[]{:S(2)}, u32[]{:S(2)}) collective-permute-start(bf16[16,256,128]{2,1,0:T(8,128)(2,1)} %collective-permute-done.12.wc1), channel_id=1, source_target_pairs={{0,1},{1,2},{2,3},{3,0},{4,5},{5,6},{6,7},{7,4},{8,9},{9,10},{10,1... | collective-permute-start | bytes 3145736 | tf_op jit(solution)/shard_map/ppermute | solution.py:473
  87.7 24.5 %collective-permute-start.18 = (bf16[512,512]{1,0:T(8,128)(2,1)S(1)}, bf16[512,512]{1,0:T(8,128)(2,1)S(1)}, u32[]{:S(2)}, u32[]{:S(2)}) collective-permute-start(bf16[512,512]{1,0:T(8,128)(2,1)S(1)} %get-tuple-element.37), channel_id=1, source_target_pairs={{0,64},{1,65},{2,66},{3,67},{4,68},{5,69},{6,70},{7,71},{8,72},{9,... | collective-permute-start | bytes 1572872 | tf_op jit(solution)/shard_map/ppermute | solution.py:478
  91.9 11.5 %all-to-all-start = ((f32[32,1,128]{2,1,0:T(1,128)}), f32[32,1,128]{2,1,0:T(1,128)S(1)}, u32[]{:S(2)}, u32[]{:S(2)}) async-start(f32[32,1,128]{2,1,0:T(1,128)} %bitcast.12), calls=%async_computation | async-start | bytes 32768 | tf_op jit(solution)/shard_map/all_to_all | solution.py:422
  103.4 0.6 copy-start.3
  105.3 13.4 %all-to-all-start.1 = ((f32[8,1,128]{2,1,0:T(1,128)}), f32[8,1,128]{2,1,0:T(1,128)S(1)}, u32[]{:S(2)}, u32[]{:S(2)}) async-start(f32[8,1,128]{2,1,0:T(1,128)} %bitcast.45), calls=%async_computation.1 | async-start | bytes 8192 | tf_op jit(solution)/shard_map/all_to_all | solution.py:422
